TPU v7x, 32 devices: a whole 2x2x4 slice. The times are simulated.
32 devices in a mesh: dp: 2 (over x), seq: 8 (over z, core), tensor: 2 (over y).
Axes of the slice: x: 2, y: 2, z: 4, core: 2. Of those that a mesh axis runs over, the one named last changes fastest.
Arguments:
- tokens: bfloat16 [2, 4096, 768], P('dp', 'seq'), may hold values from -6 to 6
- doc_ids: int32 [2, 4096], P('dp'), may hold values from 0 to 15, as said below
- memory: bfloat16 [20, 768], replicated, may hold values from -6 to 6
- qkv_weight: bfloat16 [768, 3, 768], P(None, None, 'tensor'), may hold values from -0.21875 to 0.21875
- query_bias: float32 [768], P('tensor'), may hold values from -3 to 3
- value_bias: float32 [768], P('tensor'), may hold values from -3 to 3
- out_weight: bfloat16 [768, 768], P(None, 'tensor'), may hold values from -1.75 to 1.75
- out_bias: float32 [768], replicated, may hold values from -1.75 to 1.75
- norm1_gain: float32 [768], replicated, may hold values from 0.5 to 1.5
- norm1_bias: float32 [768], replicated, may hold values from -1.75 to 1.75
- up_weight: bfloat16 [768, 3072], P(None, 'tensor'), may hold values from -0.21875 to 0.21875
- up_bias: float32 [3072], P('tensor'), may hold values from -3 to 3
- down_weight: bfloat16 [768, 3072], P(None, 'tensor'), may hold values from -0.109375 to 0.109375
- down_bias: float32 [768], replicated, may hold values from -1.75 to 1.75
- norm2_gain: float32 [768], replicated, may hold values from 0.5 to 1.5
- norm2_bias: float32 [768], replicated, may hold values from -1.75 to 1.75
- out_grad: bfloat16 [2, 4096, 768], P('dp', 'seq'), may hold values from -6 to 6
Outputs:
- output: bfloat16 [2, 4096, 768], P('dp', 'seq')
- input_grad: bfloat16 [2, 4096, 768], P('dp', 'seq')
- memory_grad: float32 [20, 768], replicated
- qkv_weight_grad: float32 [768, 3, 768], P('seq', None, 'tensor')
- query_bias_grad: float32 [768], P('tensor')
- value_bias_grad: float32 [768], P('tensor')
- out_weight_grad: float32 [768, 768], P('seq', 'tensor')
- out_bias_grad: float32 [768], P('seq')
- norm1_gain_grad: float32 [768], P('seq')
- norm1_bias_grad: float32 [768], P('seq')
- up_weight_grad: float32 [768, 3072], P('seq', 'tensor')
- up_bias_grad: float32 [3072], P('tensor')
- down_weight_grad: float32 [768, 3072], P('seq', 'tensor')
- down_bias_grad: float32 [768], P('seq')
- norm2_gain_grad: float32 [768], P('seq')
- norm2_bias_grad: float32 [768], P('seq')
Inputs may be any that keep to these rules, and one draw needn't show every extreme that they name: In every sequence doc_ids never fall, each document covers 21 to 1536 consecutive rows, every number of 0 to 15 is used, and one document has exactly 1536 rows.
All inputs are finite; a program needn't handle non-finite values.
Results may differ from a plain program's by a relative error of at most 0.024.
Values may be sent and summed in bfloat16 or wider, within the bound.
A program may use at most 192 MiB of HBM per device.

v0:
```python
import functools

import jax
import jax.numpy as jnp
from jax import lax
from jax.experimental import pallas as pl
from jax.experimental.pallas import tpu as pltpu
from jax.sharding import PartitionSpec as P

HEAD_DIM = 64
READ_ROWS = 10
REACH = 3
NORM_EPS = 1e-05
OWNERS = 4
F32, BF16 = jnp.float32, jnp.bfloat16
NT = (((1,), (1,)), ((), ()))
NN = (((1,), (0,)), ((), ()))
NEG = -1e30
FLOOR = -1e29
VMEM = pl.BlockSpec(memory_space=pltpu.VMEM)
SMEM = pl.BlockSpec(memory_space=pltpu.SMEM)


def remote(source, target, send_sem, recv_sem, **where):
    return pltpu.make_async_remote_copy(
        source, target, send_sem, recv_sem, device_id=where, device_id_type=pl.DeviceIdType.MESH
    )


def greet(partners):
    barrier = pltpu.get_barrier_semaphore()
    total = 0
    for present, where in partners:
        total = total + present.astype(jnp.int32)

        @pl.when(present)
        def _():
            pl.semaphore_signal(barrier, inc=1, device_id=where, device_id_type=pl.DeviceIdType.MESH)

    pl.semaphore_wait(barrier, total)


def dot(a, b, dims=NN):
    return lax.dot_general(a, b, dims, preferred_element_type=F32)

def low_half(shape):
    return lax.broadcasted_iota(jnp.int32, shape, len(shape) - 1) < 64

def id_columns(ids_ref, start, count):
    row = jnp.broadcast_to(ids_ref[0:1, pl.ds(start, count)], (128, count))
    return jnp.transpose(row)

def wide(x, count):
    return jnp.concatenate([x] * (count // 128), axis=1)

def split_heads(source_ref, rows, target_ref, pairs, keep):
    for pair in range(pairs):
        block = source_ref[rows, pair * 128:pair * 128 + 128]
        target_ref[2 * pair] = jnp.where(keep, block, jnp.zeros_like(block))
        target_ref[2 * pair + 1] = jnp.where(keep, jnp.zeros_like(block), block)

def sweep(rng_ref, b, body):
    first, full_first, full_last, last = (rng_ref[4 * b + i] for i in range(4))
    lax.fori_loop(full_first, full_last, lambda j, c: body(j, False, c), 0)

    def edge(i, c):
        j = first + i
        return body(jnp.where(j < full_first, j, j + full_last - full_first), True, c)

    lax.fori_loop(0, last - first - (full_last - full_first), edge, 0)

def fwd_kernel(bq, bk, own, rng_ref, q_ref, k_ref, v_ref, ids_ref, o_ref, lse_ref, acc_ref, max_ref, q_heads, cols_ref):
    pairs = q_ref.shape[1] // 128
    rows = o_ref.shape[0]
    low_q, low_k = low_half((bq, 128)), low_half((bk, 128))

    def block(qb, carry):
        mine = pl.ds(pl.multiple_of(qb * bq, bq), bq)
        cols_ref[...] = id_columns(ids_ref, pl.multiple_of(own + qb * bq, bq), bq)
        split_heads(q_ref, pl.ds(pl.multiple_of(own + qb * bq, bq), bq), q_heads, pairs, low_q)
        acc_ref[...] = jnp.zeros_like(acc_ref)
        max_ref[...] = jnp.full_like(max_ref, FLOOR)

        def step(j, masked, carry):
            there = pl.ds(pl.multiple_of(j * bk, bk), bk)
            def pair_step(pair, carry):
                lanes = pl.ds(pair * 128, 128)
                key = k_ref[there, lanes]
                value = v_ref[there, lanes]
                for odd in range(2):
                    head = 2 * pair + odd
                    scores = dot(q_heads[head], key, NT)
                    if masked:
                        scores = jnp.where(wide(cols_ref[...], bk) == ids_ref[0:1, there], scores, NEG)
                    old = max_ref[head]
                    new = jnp.maximum(old, jnp.max(scores, axis=1, keepdims=True))
                    probs = jnp.exp(scores - wide(new, bk)).astype(BF16)
                    ones = jnp.where(low_k if odd == 0 else ~low_k, value, jnp.ones_like(value))
                    acc_ref[head] = acc_ref[head] * jnp.exp(old - new) + dot(probs, ones)
                    max_ref[head] = new
                return carry
            for pair in range(pairs):
                pair_step(pair, carry)
            return carry

        sweep(rng_ref, qb, step)
        stats = jnp.zeros((bq, 128), F32)
        lane = lax.broadcasted_iota(jnp.int32, (bq, 128), 1)
        for pair in range(pairs):
            even, odd = acc_ref[2 * pair], acc_ref[2 * pair + 1]
            total_even, total_odd = even[:, 64:65], odd[:, 0:1]
            mixed = jnp.where(low_q, even / total_even, odd / total_odd)
            o_ref[mine, pair * 128:pair * 128 + 128] = mixed.astype(BF16)
            stats = jnp.where(lane == 2 * pair, max_ref[2 * pair] + jnp.log(total_even), stats)
            stats = jnp.where(lane == 2 * pair + 1, max_ref[2 * pair + 1] + jnp.log(total_odd), stats)
        lse_ref[mine, :] = stats
        return carry

    lax.fori_loop(0, rows // bq, block, 0)

def attention_forward(rng, query, key, value, ids, rows, own, bq=256, bk=256):
    width = query.shape[1]
    heads = width // 64
    return pl.pallas_call(
        functools.partial(fwd_kernel, bq, bk, own),
        out_shape=(jax.ShapeDtypeStruct((rows, width), BF16), jax.ShapeDtypeStruct((rows, 128), F32)),
        in_specs=[pl.BlockSpec(memory_space=pltpu.SMEM)] + [pl.BlockSpec(memory_space=pltpu.VMEM)] * 4,
        out_specs=(pl.BlockSpec(memory_space=pltpu.VMEM),) * 2,
        scratch_shapes=[pltpu.VMEM((heads, bq, 128), F32), pltpu.VMEM((heads, bq, 128), F32), pltpu.VMEM((heads, bq, 128), BF16), pltpu.VMEM((bq, 128), F32)],
        compiler_params=pltpu.CompilerParams(vmem_limit_bytes=24 << 20),
        name="attention_forward",
    )(rng, query, key, value, ids)

def bwd_kernel(bq, bk, own, rng_ref, q_ref, k_ref, v_ref, g_ref, ids_ref, lse_ref, along_ref, rows_ref, out_ref, dq_acc, dk_acc, dv_acc, q_heads, k_heads, v_heads, g_heads, lse_cols, along_cols, cols_ref):
    rows, width = out_ref.shape[0], q_ref.shape[1]
    pairs = width // 128
    heads = 2 * pairs
    low_q = low_half((bq, 128))

    def block(b, carry):
        start = pl.multiple_of(b * bq, bq)
        mine = pl.ds(start, bq)
        here = pl.ds(pl.multiple_of(own + start, bq), bq)
        cols_ref[...] = id_columns(ids_ref, pl.multiple_of(own + start, bq), bq)
        for source, target in ((q_ref, q_heads), (k_ref, k_heads), (v_ref, v_heads), (g_ref, g_heads)):
            split_heads(source, here, target, pairs, low_q)
        for head in range(heads):
            lse_cols[head] = jnp.broadcast_to(lse_ref[mine, head:head + 1], (bq, 128))
            along_cols[head] = jnp.broadcast_to(along_ref[mine, head:head + 1], (bq, 128))
        for acc in (dq_acc, dk_acc, dv_acc):
            acc[...] = jnp.zeros_like(acc)

        def step(j, masked, carry):
            there = pl.ds(pl.multiple_of(j * bk, bk), bk)
            def pair_step(pair, carry):
                lanes = pl.ds(pair * 128, 128)
                q_far, k_far, v_far, g_far = (r[there, lanes] for r in (q_ref, k_ref, v_ref, g_ref))
                def hide(x):
                    return jnp.where(wide(cols_ref[...], bk) == ids_ref[0:1, there], x, 0.0) if masked else x
                for odd in range(2):
                    head = 2 * pair + odd
                    scores = dot(q_heads[head], k_far, NT)
                    probs = hide(jnp.exp(scores - wide(lse_cols[head], bk)))
                    slope = dot(g_heads[head], v_far, NT)
                    grad = (probs * (slope - wide(along_cols[head], bk))).astype(BF16)
                    dq_acc[head] += dot(grad, k_far)
                    scores = dot(k_heads[head], q_far, NT)
                    probs = hide(jnp.exp(scores - rows_ref[pl.ds(head, 1), there]))
                    slope = dot(v_heads[head], g_far, NT)
                    grad = (probs * (slope - rows_ref[pl.ds(8 + head, 1), there])).astype(BF16)
                    dv_acc[head] += dot(probs.astype(BF16), g_far)
                    dk_acc[head] += dot(grad, q_far)
                return carry
            for pair in range(pairs):
                pair_step(pair, carry)
            return carry

        sweep(rng_ref, b, step)
        for which, (acc, factor) in enumerate(((dq_acc, 0.125), (dk_acc, 1.0), (dv_acc, 1.0))):
            for pair in range(pairs):
                both = jnp.where(low_q, acc[2 * pair], acc[2 * pair + 1]) * factor
                out_ref[mine, which * width + pair * 128:which * width + pair * 128 + 128] = both.astype(BF16)
        return carry

    lax.fori_loop(0, rows // bq, block, 0)

def attention_backward(rng, query, key, value, grads, ids, lse, along, stat_rows, rows, own, bq=256, bk=256):
    width = query.shape[1]
    heads = width // 64
    return pl.pallas_call(
        functools.partial(bwd_kernel, bq, bk, own),
        out_shape=jax.ShapeDtypeStruct((rows, 3 * width), BF16),
        in_specs=[pl.BlockSpec(memory_space=pltpu.SMEM)] + [pl.BlockSpec(memory_space=pltpu.VMEM)] * 8,
        out_specs=pl.BlockSpec(memory_space=pltpu.VMEM),
        scratch_shapes=[pltpu.VMEM((heads, bq, 128), F32)] * 3 + [pltpu.VMEM((heads, bq, 128), BF16)] * 4 + [pltpu.VMEM((heads, bq, 128), F32)] * 2 + [pltpu.VMEM((bq, 128), F32)],
        compiler_params=pltpu.CompilerParams(vmem_limit_bytes=40 << 20),
        name="attention_backward",
    )(rng, query, key, value, grads, ids, lse, along, stat_rows)

class Halo:
    def __init__(self, count, pieces, send_sem, recv_sem):
        self.count, self.pieces, self.send_sem, self.recv_sem = count, pieces, send_sem, recv_sem
        s = self.s = lax.axis_index("seq")
        self.core = lax.rem(s, 2)
        self.sibling = s + 1 - 2 * self.core
        self.left, self.right = s >= 2, s < count - 2

    def greet(self):
        s, count = self.s, self.count
        greet([(s >= k, {"seq": s - k}) for k in (1, 2)] + [(s < count - k, {"seq": s + k}) for k in (1, 2)])

    def own(self, part, kind, slot, target):
        source, window = self.pieces[part]
        return remote(source, window(slot), self.send_sem.at[kind, part], self.recv_sem.at[slot, part], seq=target)

    def moved(self, part, kind, held, slot, target):
        window = self.pieces[part][1]
        return remote(window(held), window(slot), self.send_sem.at[kind, part], self.recv_sem.at[slot, part], seq=target)

    def first_copies(self, part):
        s, core = self.s, self.core
        return (
            (self.right, self.own(part, 0, 1, s + 2)),
            (self.left, self.own(part, 1, 5, s - 2)),
            (core == 0, self.own(part, 2, 2, self.sibling)),
            (core == 1, self.own(part, 2, 4, self.sibling)),
        )

    def from_left(self, part):
        s, core, left, right = self.s, self.core, self.left, self.right
        return (
            (jnp.logical_and(left, jnp.logical_and(core == 1, right)), self.moved(part, 3, 1, 0, s + 1)),
            (jnp.logical_and(left, core == 0), self.moved(part, 4, 1, 0, self.sibling)),
            (jnp.logical_and(left, core == 1), self.moved(part, 4, 1, 2, self.sibling)),
        )

    def from_right(self, part):
        s, core, left, right = self.s, self.core, self.left, self.right
        return (
            (jnp.logical_and(right, jnp.logical_and(core == 0, left)), self.moved(part, 5, 5, 6, s - 1)),
            (jnp.logical_and(right, core == 0), self.moved(part, 6, 5, 4, self.sibling)),
            (jnp.logical_and(right, core == 1), self.moved(part, 6, 5, 6, self.sibling)),
        )

    def each(self, copies, act):
        for present, copy in copies:
            pl.when(present)(functools.partial(act, copy))

    def send(self, part):
        self.each(self.first_copies(part), lambda copy: copy.start())

    def arrived(self, slot, part):
        self.own(part, 0, slot, self.s).wait_recv()

    def relay(self, part):
        pl.when(self.left)(functools.partial(self.arrived, 1, part))
        self.each(self.from_left(part), lambda copy: copy.start())
        pl.when(self.right)(functools.partial(self.arrived, 5, part))
        self.each(self.from_right(part), lambda copy: copy.start())

    def present(self, slot):
        block = self.s + slot - REACH
        return jnp.logical_and(block >= 0, block < self.count)

    def receive(self, slot):
        for part in range(len(self.pieces)):
            pl.when(self.present(slot))(functools.partial(self.arrived, slot, part))

    def finish(self):
        for part in range(len(self.pieces)):
            self.each(self.first_copies(part) + self.from_left(part) + self.from_right(part), lambda copy: copy.wait_send())


def project_kernel(count, parts, own_ref, slots_ref, memory_ref, weight_ref, query_bias_ref, value_bias_ref,
                   q_ref, k_ref, v_ref, source_ref, window_ref, send_sem, recv_sem):
    block = own_ref.shape[0]
    rows = block // parts
    tile = 256
    tiles = block // tile

    def piece(part):
        return own_ref.at[pl.ds(part * rows, rows)], lambda slot: window_ref.at[pl.ds(slot * block + part * rows, rows)]

    halo = Halo(count, [piece(part) for part in range(parts)], send_sem, recv_sem)
    halo.greet()
    for part in range(parts):
        halo.send(part)

    def project(load, start, keep):
        hot = (lax.broadcasted_iota(jnp.int32, (32, tile), 0) == slots_ref[0:1, pl.ds(start, tile)]).astype(F32).astype(BF16)
        tn = (((0,), (0,)), ((), ()))
        chosen = dot(hot, memory_ref[...], tn)
        inside = wide(dot(hot, jnp.ones((32, 128), BF16), tn), chosen.shape[1])
        source = jnp.where(inside > 0.5, chosen, load().astype(F32)).astype(BF16)
        keep(source)
        out = pl.ds(start, tile)
        q_ref[out, :] = (dot(source, weight_ref[0]) + query_bias_ref[...]).astype(BF16) * 0.125
        k_ref[out, :] = dot(source, weight_ref[1]).astype(BF16)
        v_ref[out, :] = (dot(source, weight_ref[2]) + value_bias_ref[...]).astype(BF16)

    def own_tile(i, carry):
        at = pl.ds(pl.multiple_of(i * tile, tile), tile)

        def keep(source):
            source_ref[at, :] = source

        project(lambda: own_ref[at, :], pl.multiple_of(REACH * block + i * tile, tile), keep)
        return carry

    lax.fori_loop(0, tiles, own_tile, 0)
    for part in range(parts):
        halo.relay(part)

    def two_blocks(low, high):
        def step(i, carry):
            slot = low + (high - low) * (i // tiles)

            @pl.when(halo.present(slot))
            def _():
                start = pl.multiple_of(slot * block + lax.rem(i, tiles) * tile, tile)
                project(lambda: window_ref[pl.ds(start, tile), :], start, lambda source: None)

            return carry

        lax.fori_loop(0, 2 * tiles, step, 0)

    two_blocks(1, 5)
    for slots in ((2, 4), (0, 6)):
        for slot in slots:
            halo.receive(slot)
        two_blocks(*slots)
    halo.finish()


def project_window(own, slots, memory, weight, query_bias, value_bias, count, collective_id, parts=2):
    rows, dim = own.shape
    width = weight.shape[2]
    total = (2 * REACH + 1) * rows
    wide_out = jax.ShapeDtypeStruct((total, width), BF16)
    return pl.pallas_call(
        functools.partial(project_kernel, count, parts),
        out_shape=(wide_out, wide_out, wide_out, jax.ShapeDtypeStruct((rows, dim), BF16)),
        in_specs=[VMEM] * 6,
        out_specs=(VMEM,) * 4,
        scratch_shapes=[
            pltpu.VMEM((total, dim), BF16),
            pltpu.SemaphoreType.DMA((7, parts)),
            pltpu.SemaphoreType.DMA((7, parts)),
        ],
        compiler_params=pltpu.CompilerParams(collective_id=collective_id, has_side_effects=True, vmem_limit_bytes=40 << 20),
        name="project_window",
    )(own, slots, memory, weight, query_bias, value_bias)


def grads_kernel(count, parts, grad_ref, mixed_ref, lse_ref, low_ref, window_ref, stats_ref, along_ref, out_grad_ref, own_stats, send_sem, recv_sem):
    block, width = grad_ref.shape
    rows = block // parts

    def piece(part):
        return grad_ref.at[pl.ds(part * rows, rows)], lambda slot: window_ref.at[pl.ds(slot * block + part * rows, rows)]

    stats_piece = own_stats, lambda slot: stats_ref.at[:, pl.ds(slot * block, block)]
    halo = Halo(count, [piece(part) for part in range(parts)] + [stats_piece], send_sem, recv_sem)
    halo.greet()
    for part in range(parts):
        halo.send(part)
    window_ref[REACH * block:(REACH + 1) * block, :] = grad_ref[...]
    lane = lax.broadcasted_iota(jnp.int32, (block, 128), 1)
    along = jnp.zeros((block, 128), F32)
    for pair in range(width // 128):
        lanes = slice(pair * 128, pair * 128 + 128)
        product = grad_ref[:, lanes].astype(F32) * mixed_ref[:, lanes].astype(F32)
        even = jnp.sum(jnp.where(lane < 64, product, 0.0), axis=1, keepdims=True)
        odd = jnp.sum(jnp.where(lane < 64, 0.0, product), axis=1, keepdims=True)
        along = jnp.where(lane == 2 * pair, even, jnp.where(lane == 2 * pair + 1, odd, along))
    along_ref[...] = along
    own_stats[0:8, :] = jnp.transpose(lse_ref[...])[0:8, :]
    own_stats[8:16, :] = jnp.transpose(along)[0:8, :]
    stats_ref[:, REACH * block:(REACH + 1) * block] = own_stats[...]
    halo.send(parts)
    out_grad_ref[...] = dot(low_ref[...], mixed_ref[...], (((0,), (0,)), ((), ()))).astype(BF16)
    for part in range(parts + 1):
        halo.relay(part)
    for slot in (0, 2, 4, 6):
        halo.receive(slot)
    halo.finish()


def gather_grads(grad, mixed, lse, low, count, collective_id, parts=2):
    rows, width = grad.shape
    total = (2 * REACH + 1) * rows
    return pl.pallas_call(
        functools.partial(grads_kernel, count, parts),
        out_shape=(
            jax.ShapeDtypeStruct((total, width), BF16),
            jax.ShapeDtypeStruct((16, total), F32),
            jax.ShapeDtypeStruct((rows, 128), F32),
            jax.ShapeDtypeStruct((low.shape[1], width), BF16),
        ),
        in_specs=[VMEM] * 4,
        out_specs=(VMEM,) * 4,
        scratch_shapes=[
            pltpu.VMEM((16, rows), F32),
            pltpu.SemaphoreType.DMA((7, parts + 1)),
            pltpu.SemaphoreType.DMA((7, parts + 1)),
        ],
        compiler_params=pltpu.CompilerParams(collective_id=collective_id, has_side_effects=True, vmem_limit_bytes=24 << 20),
        name="gather_grads",
    )(grad, mixed, lse, low)


def split_dot(left, right, dims):
    high = right.astype(BF16)
    low = (right - high.astype(F32)).astype(BF16)
    return dot(left, high, dims) + dot(left, low, dims)


def tail_kernel(dps, seqs, width, *refs):
    (early_refs, (out_grad_ref, proj_ref, source_ref, weight_ref, input1_ref, select_ref, small_ref),
     (up_out, down_out, out_out, qkv_out, input_out, small_out),
     (mix, y_send, y_recv, a_recv, parts, b_recv, small_in, small_recv, small_mine, small_dp),
     (mine, c_recv, last, d_recv), (y_sems, a_sems, b_sems, c_sems, d_sems, s_sems)) = (
        refs[:dps], refs[dps:dps + 7], refs[dps + 7:dps + 13], refs[dps + 13:dps + 23], refs[dps + 23:dps + 27], refs[dps + 27:])
    zs = seqs // 2
    bits = zs.bit_length() - 1
    t, d, s = lax.axis_index("tensor"), lax.axis_index("dp"), lax.axis_index("seq")
    z, core = s // 2, lax.rem(s, 2)
    sibling = s + 1 - 2 * core
    late, early = a_recv.shape[0], mine.shape[0] - a_recv.shape[0]
    chunk = a_recv.shape[3]
    shares = -(-chunk // width)
    owners = small_out.shape[0]
    block, hidden = up_out.shape
    share_width = early * width
    rows, columns = proj_ref.shape
    third = columns // 3
    steps = y_send.shape[0]
    span = rows // steps
    true = s >= 0
    partners = [(true, {"seq": lax.rem(s + k, seqs)}) for k in range(1, seqs)]
    partners += [(true, {"dp": lax.rem(d + k, dps)}) for k in range(1, dps)]
    partners += [(true, {"tensor": 1 - t})]
    greet(partners)

    def active(c):
        return true if c < early else d < shares

    def a_copy(c, j):
        start = pl.multiple_of((2 * j + 1 - core) * block, 16)
        at = (c - early) * chunk
        i = c - early
        return remote(mix.at[pl.ds(start, block), pl.ds(at, chunk)], a_recv.at[i, j], a_sems.at[0, i, j], a_sems.at[1, i, j], seq=sibling)

    def b_copy(c, k):
        other = lax.rem(d + k, dps)
        i = c - early
        return other, remote(parts.at[i, other], b_recv.at[i, k], b_sems.at[0, i, k], b_sems.at[1, i, k], dp=other)

    def first_slot(b):
        return sum(zs // (2 << e) for e in range(b))

    def c_copies(c, b):
        size = 2 << b
        high = lax.rem(z // (1 << b), 2)
        partner = z + (1 << b) - (size * high)
        low = lax.rem(partner, size)
        return [
            remote(mine.at[c, i * size + low], c_recv.at[c, first_slot(b) + i], c_sems.at[0, c, first_slot(b) + i], c_sems.at[1, c, first_slot(b) + i], seq=2 * partner + core)
            for i in range(zs // size)
        ]

    def d_copy(c, k):
        return remote(last.at[c], d_recv.at[c, k], d_sems.at[0, c, k], d_sems.at[1, c, k], dp=lax.rem(d + k, dps))

    def start_a(c):
        for j in range(zs):
            a_copy(c, j).start()

    def start_early(c):
        lanes = slice(c * width, c * width + width)
        for j in range(zs):
            total = early_refs[0][0, j, :, lanes].astype(F32)
            for k in range(1, dps):
                total = total + early_refs[k][j, :, lanes].astype(F32)
            mine[c, j] = total.astype(BF16)
        for copy in c_copies(c, 0):
            copy.start()

    def end_a(c):
        i = c - early
        for j in range(zs):
            a_copy(c, j).wait()
            start = pl.multiple_of((2 * j + core) * block, 16)
            for p in range(shares):
                real = min(width, chunk - p * width)
                lanes = pl.ds(i * chunk + p * width, real)
                total = mix[pl.ds(start, block), lanes].astype(F32) + a_recv[i, j, :, p * width:p * width + real].astype(F32)
                parts[i, p, j, :, 0:real] = total.astype(BF16)
                if real < width:
                    parts[i, p, j, :, real:width] = jnp.zeros((block, width - real), BF16)
        for k in range(1, dps):
            other, copy = b_copy(c, k)
            pl.when(other < shares)(copy.start)

    def end_b(c):
        i = c - early
        for k in range(1, dps):
            other, copy = b_copy(c, k)
            pl.when(other < shares)(copy.wait_send)

        @pl.when(d < shares)
        def _():
            for k in range(1, dps):
                b_copy(c, k)[1].wait_recv()
            for j in range(zs):
                total = parts[i, d, j].astype(F32)
                for k in range(1, dps):
                    total = total + b_recv[i, k, j].astype(F32)
                mine[c, j] = total.astype(BF16)
            for copy in c_copies(c, 0):
                copy.start()

    def end_c(c, b):
        size = 2 << b
        kept = lax.rem(z, size)

        @pl.when(active(c))
        def _():
            for i, copy in enumerate(c_copies(c, b)):
                copy.wait()
                held = mine[c, i * size + kept].astype(F32) + c_recv[c, first_slot(b) + i].astype(F32)
                if b < bits - 1:
                    mine[c, i * size + kept] = held.astype(BF16)
                else:
                    last[c] = held.astype(BF16)
            if b < bits - 1:
                for copy in c_copies(c, b + 1):
                    copy.start()
            else:
                for k in range(1, dps):
                    d_copy(c, k).start()

    def put(c, share, value):
        count = dps if c < early else shares
        for p in range(count):

            @pl.when(share == p)
            def _():
                if c < early:
                    which, column = divmod(p * share_width + c * width, hidden)
                    (up_out, down_out)[which][:, column:column + width] = value.astype(F32)
                    return
                first = (c - early) * chunk + p * width
                for lane in range(0, min(width, chunk - p * width), 128):
                    which, column = divmod(first + lane, third)
                    part = value[:, lane:lane + 128].astype(F32)
                    if which == 0:
                        out_out[:, column:column + 128] = part
                    else:
                        qkv_out[which - 1, :, column:column + 128] = part

    def end_d(c):
        @pl.when(active(c))
        def _():
            put(c, d, last[c])
            for k in range(1, dps):
                d_copy(c, k).wait_send()

        for k in range(1, dps):
            share = lax.rem(d + dps - k, dps)

            @pl.when(true if c < early else share < shares)
            def _():
                d_copy(c, k).wait_recv()
                put(c, share, d_recv[c, k])

    def y_copy(i):
        return remote(y_send.at[i], y_recv.at[i], y_sems.at[0, i], y_sems.at[1, i], tensor=1 - t)

    for c in range(early):
        start_early(c)
    out_width = out_grad_ref.shape[1]
    mix[:, 0:out_width] = out_grad_ref[...]
    for i in range(3):
        part = lax.dot_general(source_ref[...], proj_ref[:, i * third:(i + 1) * third], (((0,), (0,)), ((), ())), preferred_element_type=F32)
        mix[:, out_width + i * third:out_width + (i + 1) * third] = part.astype(BF16)
    for c in range(early, early + late):
        start_a(c)
    for i in range(steps):
        at = slice(i * span, (i + 1) * span)
        y_send[i] = sum(dot(proj_ref[at, j * third:(j + 1) * third], weight_ref[j], NT) for j in range(3)).astype(BF16)
        y_copy(i).start()
    small_in[0] = small_ref[...]
    for i in range(1, owners):
        small_in[i] = jnp.zeros_like(small_ref)
    small_in[1, 0:1, 0:third] = jnp.sum(proj_ref[:, 0:third].astype(F32), axis=0, keepdims=True)
    small_in[1, 0:1, third:2 * third] = jnp.sum(proj_ref[:, 2 * third:3 * third].astype(F32), axis=0, keepdims=True)

    def end_y():
        memory = jnp.zeros((32, input_out.shape[1]), F32)
        for i in range(steps):
            y_copy(i).wait()
            at = slice(i * span, (i + 1) * span)
            total = input1_ref[at, :] + (y_send[i].astype(F32) + y_recv[i].astype(F32))
            select = select_ref[at, :]
            memory = memory + split_dot(select, total, (((0,), (0,)), ((), ())))
            inside = dot(select, jnp.ones((32, total.shape[1]), BF16))
            input_out[at, :] = jnp.where(inside > 0.5, 0.0, total).astype(BF16)
        small_in[1, 1:8, :] = memory[0:7]
        small_in[2] = memory[7:15]
        small_in[3, 0:5, :] = memory[15:20]
        for hop in range(1, seqs):
            owner = lax.rem(s + hop, seqs)
            pl.when(owner < owners)(to_owner(hop, owner).start)

    def to_owner(hop, owner):
        return remote(small_in.at[owner], small_recv.at[hop], s_sems.at[0, 0, hop], s_sems.at[1, 0, hop], seq=owner)

    def across(k):
        return remote(small_mine, small_dp.at[k], s_sems.at[0, 1, k], s_sems.at[1, 1, k], dp=lax.rem(d + k, dps))

    def back(hop, owner, target):
        return remote(small_out.at[owner], small_out.at[owner], s_sems.at[0, 2, hop], s_sems.at[1, 2, hop], seq=target)

    def small_one():
        @pl.when(s < owners)
        def _():
            total = small_in[s]
            for hop in range(1, seqs):
                to_owner(hop, s).wait_recv()
                total = total + small_recv[hop]
            small_mine[...] = total
            for k in range(1, dps):
                across(k).start()

    def small_two():
        @pl.when(s < owners)
        def _():
            small_dp[0] = small_mine[...]
            for k in range(1, dps):
                across(k).wait()
            ordered = jnp.zeros(small_mine.shape, F32)
            for index in range(dps):
                ordered = ordered + small_dp[lax.rem(d + dps - index, dps)]
            small_out[s] = ordered
            for hop in range(1, seqs):
                back(hop, s, lax.rem(s + hop, seqs)).start()

    def small_three():
        for hop in range(1, seqs):
            owner = lax.rem(s + hop, seqs)
            pl.when(owner < owners)(to_owner(hop, owner).wait_send)
        for hop in range(1, seqs):
            pl.when(lax.rem(s + seqs - hop, seqs) < owners)(back(hop, 0, s).wait_recv)
            pl.when(s < owners)(back(hop, 0, s).wait_send)

    zed = [functools.partial(end_c, b=b) for b in range(bits)]
    lates = list(range(early, early + late))
    for c in lates:
        end_a(c)
    for c in range(early):
        zed[0](c)
    for c in lates:
        end_b(c)
    end_y()
    for b in range(1, bits):
        for c in range(early):
            zed[b](c)
        for c in lates:
            zed[b - 1](c)
        if b == 1:
            small_one()
    for c in range(early):
        end_d(c)
    small_two()
    for c in lates:
        zed[bits - 1](c)
    for c in lates:
        end_d(c)
    small_three()


def tail(early, out, proj, source, weight, input1, select, small, dps, seqs):
    zs = seqs // 2
    dim = source.shape[1]
    hidden = early[0].shape[3] * dps // 2
    rows = proj.shape[0]
    block = dim // seqs
    mixed = out.shape[1] + proj.shape[1]
    late = 2
    chunk = mixed // late
    width = -(-chunk // (128 * dps)) * 128
    width = early[0].shape[3] if early[0].shape[3] % width else width
    chunks = early[0].shape[3] // width + late
    steps = 4
    table = (OWNERS,) + small.shape
    dma = pltpu.SemaphoreType.DMA
    return pl.pallas_call(
        functools.partial(tail_kernel, dps, seqs, width),
        out_shape=(
            jax.ShapeDtypeStruct((block, hidden), F32),
            jax.ShapeDtypeStruct((block, hidden), F32),
            jax.ShapeDtypeStruct((block, out.shape[1]), F32),
            jax.ShapeDtypeStruct((3, block, out.shape[1]), F32),
            jax.ShapeDtypeStruct((rows, dim), BF16),
            jax.ShapeDtypeStruct(table, F32),
        ),
        in_specs=[VMEM] * (dps + 7),
        out_specs=(VMEM,) * 6,
        scratch_shapes=[
            pltpu.VMEM((dim, mixed), BF16),
            pltpu.VMEM((steps, rows // steps, dim), BF16),
            pltpu.VMEM((steps, rows // steps, dim), BF16),
            pltpu.VMEM((late, zs, block, chunk), BF16),
            pltpu.VMEM((late, dps, zs, block, width), BF16),
            pltpu.VMEM((late, dps, zs, block, width), BF16),
            pltpu.VMEM(table, F32),
            pltpu.VMEM((seqs,) + small.shape, F32),
            pltpu.VMEM(small.shape, F32),
            pltpu.VMEM((dps,) + small.shape, F32),
            pltpu.VMEM((chunks, zs, block, width), BF16),
            pltpu.VMEM((chunks, zs - 1, block, width), BF16),
            pltpu.VMEM((chunks, block, width), BF16),
            pltpu.VMEM((chunks, dps, block, width), BF16),
            dma((2, steps)),
            dma((2, late, zs)),
            dma((2, late, dps)),
            dma((2, chunks, zs)),
            dma((2, chunks, dps)),
            dma((2, 3, max(seqs, dps))),
        ],
        compiler_params=pltpu.CompilerParams(collective_id=7, has_side_effects=True, vmem_limit_bytes=48 << 20),
        name="tail",
    )(*early, out, proj, source, weight, input1, select, small)


def feed_kernel(dps, seqs, span, mixed_ref, out_ref, other_ref, source_ref, up_ref, down_ref, vec_ref, grad_ref,
                y_ref, input1_ref, low_ref, mixed_grad_ref, shares_ref, small_ref,
                out_all, mixed_all, first_ref, hat_ref, scale_ref, first_low, act_ref, slope_ref, second_ref, down_grad, up_grad,
                y_send, y_recv, z_send, z_recv, grads, a_recv, m_sems, y_sems, z_sems, a_sems):
    rows, dim = source_ref.shape
    width, hidden = mixed_ref.shape[1], up_ref.shape[1]
    zs, block = seqs // 2, dim // seqs
    t, d, s = lax.axis_index("tensor"), lax.axis_index("dp"), lax.axis_index("seq")
    core = lax.rem(s, 2)
    sibling = s + 1 - 2 * core
    spans = rows // span
    true = s >= 0
    greet([(true, {"tensor": 1 - t}), (true, {"seq": sibling})])
    tn = (((0,), (0,)), ((), ()))

    def at(i):
        return pl.ds(pl.multiple_of(i * span, span), span)

    mine = pl.ds(pl.multiple_of(t * width, 128), width)
    theirs = pl.ds(pl.multiple_of((1 - t) * width, 128), width)

    def m_copy(i):
        return remote(mixed_ref.at[at(i)], mixed_all.at[at(i), mine], m_sems.at[0, i], m_sems.at[1, i], tensor=1 - t)

    def y_copy(i):
        return remote(y_send.at[at(i)], y_recv.at[at(i)], y_sems.at[0, i], y_sems.at[1, i], tensor=1 - t)

    def z_copy(i):
        return remote(z_send.at[at(i)], z_recv.at[at(i)], z_sems.at[0, i], z_sems.at[1, i], tensor=1 - t)

    def a_copy(which, j):
        start = pl.multiple_of((2 * j + 1 - core) * block, 16)
        return remote(grads.at[which, pl.ds(start, block)], a_recv.at[which, j], a_sems.at[0, which, j], a_sems.at[1, which, j], seq=sibling)

    def mean(x):
        return jnp.mean(x, axis=1, keepdims=True)

    def norm(x):
        centred = x - mean(x)
        scale = lax.rsqrt(mean(centred * centred) + NORM_EPS)
        return centred * scale, scale

    def norm_back(grad, hat, scale, gain):
        grad = grad * gain
        return scale * (grad - mean(grad) - hat * mean(grad * hat))

    def add_rows(row, x):
        small_ref[row:row + 1, :] += jnp.sum(x, axis=0, keepdims=True)

    out_bias, gain1, shift1, down_bias, gain2, shift2 = (vec_ref[i:i + 1, :] for i in range(6))

    for i in range(spans):
        m_copy(i).start()
    out_all[:, mine] = out_ref[...]
    out_all[:, theirs] = other_ref[...]
    mixed_all[:, mine] = mixed_ref[...]
    small_ref[...] = jnp.zeros_like(small_ref)

    def forward(i, carry):
        m_copy(i).wait()
        branch = dot(mixed_all[at(i), :], out_all[...], NT) + out_bias
        hat, scale = norm(source_ref[at(i), :].astype(F32) + branch)
        first = hat * gain1 + shift1
        low = first.astype(BF16)
        hat_ref[at(i), :] = hat
        scale_ref[at(i), :] = jnp.broadcast_to(scale, (span, 128))
        first_ref[at(i), :] = first
        first_low[at(i), :] = low
        part = jnp.zeros((span, dim), F32)
        for k in range(2):
            cols = slice(k * dim, (k + 1) * dim)
            up = dot(low, up_ref[:, cols]) + vec_ref[6 + k:7 + k, :]
            below = 0.5 + 0.5 * lax.erf(up * 0.7071067811865476)
            act = (up * below).astype(BF16)
            slope_ref[at(i), cols] = below + up * jnp.exp(-0.5 * up * up) * 0.3989422804014327
            act_ref[at(i), cols] = act
            part = part + dot(act, down_ref[:, cols], NT)
        y_send[at(i), :] = part.astype(BF16)
        y_copy(i).start()
        return carry

    lax.fori_loop(0, spans, forward, 0)

    def turn(i, carry):
        y_copy(i).wait()
        down = y_send[at(i), :].astype(F32) + y_recv[at(i), :].astype(F32) + down_bias
        hat, scale = norm(first_ref[at(i), :] + down)
        y_ref[at(i), :] = (hat * gain2 + shift2).astype(BF16)
        grad = grad_ref[at(i), :].astype(F32)
        add_rows(2, grad * hat)
        add_rows(3, grad)
        second = norm_back(grad, hat, scale, gain2)
        low = second.astype(BF16)
        second_ref[at(i), :] = second
        down_grad[at(i), :] = low
        add_rows(5, low.astype(F32))
        part = jnp.zeros((span, dim), F32)
        for k in range(2):
            cols = slice(k * dim, (k + 1) * dim)
            up = (slope_ref[at(i), cols] * dot(low, down_ref[:, cols])).astype(BF16)
            up_grad[at(i), cols] = up
            add_rows(6 + k, up.astype(F32))
            part = part + dot(up, up_ref[:, cols], NT)
        z_send[at(i), :] = part.astype(BF16)
        z_copy(i).start()
        return carry

    lax.fori_loop(0, spans, turn, 0)

    def products(j, carry):
        cols = pl.ds(pl.multiple_of(j * 512, 512), 512)
        grads[0, :, cols] = dot(first_low[...], up_grad[:, cols], tn).astype(BF16)
        grads[1, :, cols] = dot(down_grad[...], act_ref[:, cols], tn).astype(BF16)
        return carry

    lax.fori_loop(0, hidden // 512, products, 0)
    for which in range(2):
        for j in range(zs):
            a_copy(which, j).start()

    def back(i, carry):
        z_copy(i).wait()
        grad = second_ref[at(i), :] + (z_send[at(i), :].astype(F32) + z_recv[at(i), :].astype(F32))
        hat = hat_ref[at(i), :]
        add_rows(0, grad * hat)
        add_rows(1, grad)
        total = norm_back(grad, hat, scale_ref[at(i), 0:1], gain1)
        low = total.astype(BF16)
        input1_ref[at(i), :] = total
        low_ref[at(i), :] = low
        add_rows(4, low.astype(F32))
        mixed_grad_ref[at(i), :] = dot(low, out_ref[...]).astype(BF16)
        return carry

    lax.fori_loop(0, spans, back, 0)
    share = 2 * hidden // dps
    for which in range(2):
        for j in range(zs):
            a_copy(which, j).wait()
            own = pl.ds(pl.multiple_of((2 * j + core) * block, 16), block)
            for p in range(dps):
                if p * share // hidden <= which <= ((p + 1) * share - 1) // hidden:
                    first, last = max(p * share, which * hidden), min((p + 1) * share, (which + 1) * hidden)
                    cols = slice(first - which * hidden, last - which * hidden)
                    total = grads[which, own, cols].astype(F32) + a_recv[which, j, :, cols].astype(F32)
                    shares_ref[lax.rem(p - d + dps, dps), j, :, first - p * share:last - p * share] = total.astype(BF16)


def feed_forward(mixed, out_weight, out_other, source, up, down, vectors, grad, dps, seqs, span=256):
    rows, dim = source.shape
    width, hidden = mixed.shape[1], up.shape[1]
    zs, block = seqs // 2, dim // seqs
    spans = rows // span
    dma = pltpu.SemaphoreType.DMA
    return pl.pallas_call(
        functools.partial(feed_kernel, dps, seqs, span),
        out_shape=(
            jax.ShapeDtypeStruct((rows, dim), BF16),
            jax.ShapeDtypeStruct((rows, dim), F32),
            jax.ShapeDtypeStruct((rows, dim), BF16),
            jax.ShapeDtypeStruct((rows, width), BF16),
            jax.ShapeDtypeStruct((dps, zs, block, 2 * hidden // dps), BF16),
            jax.ShapeDtypeStruct((8, dim), F32),
        ),
        in_specs=[VMEM] * 8,
        out_specs=(VMEM,) * 6,
        scratch_shapes=[
            pltpu.VMEM((dim, 2 * width), BF16),
            pltpu.VMEM((rows, 2 * width), BF16),
            pltpu.VMEM((rows, dim), F32),
            pltpu.VMEM((rows, dim), F32),
            pltpu.VMEM((rows, 128), F32),
            pltpu.VMEM((rows, dim), BF16),
            pltpu.VMEM((rows, hidden), BF16),
            pltpu.VMEM((rows, hidden), F32),
            pltpu.VMEM((rows, dim), F32),
            pltpu.VMEM((rows, dim), BF16),
            pltpu.VMEM((rows, hidden), BF16),
            pltpu.VMEM((rows, dim), BF16),
            pltpu.VMEM((rows, dim), BF16),
            pltpu.VMEM((rows, dim), BF16),
            pltpu.VMEM((rows, dim), BF16),
            pltpu.VMEM((2, dim, hidden), BF16),
            pltpu.VMEM((2, zs, block, hidden), BF16),
            dma((2, spans)),
            dma((2, spans)),
            dma((2, spans)),
            dma((2, 2, zs)),
        ],
        compiler_params=pltpu.CompilerParams(collective_id=3, has_side_effects=True, vmem_limit_bytes=56 << 20),
        name="feed_forward",
    )(mixed, out_weight, out_other, source, up, down, vectors, grad)


def memory_slots(id_row):
    count = id_row.shape[0]
    edge = jnp.full((READ_ROWS,), -1, jnp.int32)
    padded = jnp.concatenate([edge, id_row, edge])
    before = sum((padded[READ_ROWS - k:READ_ROWS - k + count] == id_row).astype(jnp.int32) for k in range(1, READ_ROWS + 1))
    behind = sum((padded[READ_ROWS + k:READ_ROWS + k + count] == id_row).astype(jnp.int32) for k in range(1, READ_ROWS + 1))
    return jnp.where(before < READ_ROWS, before, jnp.where(behind < READ_ROWS, 2 * READ_ROWS - 1 - behind, -1))


def document_blocks(id_row, own_ids, window_start, bk):
    bounds = jnp.stack([own_ids[0], own_ids[-1] + 1])
    start_end = jnp.sum((id_row[None, :] < bounds[:, None]).astype(jnp.int32), axis=1) - window_start
    shift = bk.bit_length() - 1
    floor, ceil = start_end >> shift, (start_end + bk - 1) >> shift
    first, last = floor[0], ceil[1]
    whole = jnp.logical_and(bounds[0] + 1 == bounds[1], ceil[0] < floor[1])
    inside = jnp.where(whole, jnp.stack([ceil[0], floor[1]]), first)
    return jnp.concatenate([floor[:1], inside, ceil[1:]]).astype(jnp.int32)


def on_device(dps, seqs, tokens, doc_ids, memory, qkv_weight, query_bias, value_bias, out_weight, out_bias, norm1_gain, norm1_bias, up_weight, up_bias, down_weight, down_bias, norm2_gain, norm2_bias, out_grad):
    rows = tokens.shape[1]
    width = qkv_weight.shape[2]
    heads = width // HEAD_DIM
    bq, bk = rows, 256
    own = REACH * rows
    pieces = 2 * REACH + 1
    s = lax.axis_index("seq")
    id_row = doc_ids[0]
    edge = jnp.full((own,), -1, jnp.int32)
    window_start = s * rows - own
    slots = memory_slots(id_row)
    window_slots = lax.dynamic_slice_in_dim(jnp.concatenate([edge, slots, edge]), s * rows, pieces * rows, 0)
    window_ids = lax.dynamic_slice_in_dim(jnp.concatenate([edge, id_row, edge]), s * rows, pieces * rows, 0)
    own_ids = window_ids[own:own + rows]
    blocks = document_blocks(id_row, own_ids, window_start, bk)
    ids = jnp.broadcast_to(window_ids.astype(F32)[None], (8, pieces * rows))

    out_other = lax.ppermute(out_weight, "tensor", [(0, 1), (1, 0)])
    weight = qkv_weight.transpose(1, 0, 2)
    slots_row = jnp.broadcast_to(window_slots[None], (8, pieces * rows))
    memory_pad = jnp.pad(memory, ((0, 32 - memory.shape[0]), (0, 0)))
    query, key, value, source = project_window(
        tokens[0], slots_row, memory_pad, weight, query_bias[None], value_bias[None], seqs, 1)
    own_slots = window_slots[own:own + rows]

    mixed_low, logsums = attention_forward(blocks, query, key, value, ids, rows, own, bq, bk)

    vectors = jnp.stack([out_bias, norm1_gain, norm1_bias, down_bias, norm2_gain, norm2_bias, up_bias[:2 * width], up_bias[2 * width:]])
    output, grad_input1, branch_grad, mixed_grad, shares, small = feed_forward(
        mixed_low, out_weight, out_other, source, up_weight, down_weight, vectors, out_grad[0], dps, seqs)
    early = [shares] + [
        lax.ppermute(shares[k], "dp", [(i, (i + k) % dps) for i in range(dps)]) for k in range(1, dps)]
    grads_window, stats_window, along_cols, grad_out_weight = gather_grads(mixed_grad, mixed_low, logsums, branch_grad, seqs, 2)
    proj_grad = attention_backward(blocks, query, key, value, grads_window, ids, logsums, along_cols, stats_window, rows, own, bq, bk)

    select = (own_slots[:, None] == jnp.arange(32, dtype=jnp.int32)[None, :]).astype(BF16)
    up_sum, down_sum, out_sum, qkv_sum, input_grad, small = tail(
        early, grad_out_weight, proj_grad, source, weight, grad_input1, select, small, dps, seqs)
    small = small.reshape(32, 2 * width)
    input_grad = input_grad[None]
    piece = small.shape[1] // seqs
    vectors = lax.dynamic_slice_in_dim(small[:6], s * piece, piece, 1)
    memory_grad = small[9:29]
    return (
        output[None], input_grad, memory_grad,
        qkv_sum.transpose(1, 0, 2), small[8, :width], small[8, width:],
        out_sum, vectors[4], vectors[0], vectors[1],
        up_sum, small[6:8].reshape(-1), down_sum, vectors[5], vectors[2], vectors[3],
    )


def solution(mesh):
    in_specs = (
        P("dp", "seq", None), P("dp", None), P(), P(None, None, "tensor"), P("tensor"), P("tensor"), P(None, "tensor"), P(), P(), P(),
        P(None, "tensor"), P("tensor"), P(None, "tensor"), P(), P(), P(), P("dp", "seq", None),
    )
    out_specs = (
        P("dp", "seq", None), P("dp", "seq", None), P(), P("seq", None, "tensor"), P("tensor"), P("tensor"), P("seq", "tensor"), P("seq"), P("seq"), P("seq"),
        P("seq", "tensor"), P("tensor"), P("seq", "tensor"), P("seq"), P("seq"), P("seq"),
    )
    step = functools.partial(on_device, mesh.shape["dp"], mesh.shape["seq"])
    return jax.shard_map(step, mesh=mesh, in_specs=in_specs, out_specs=out_specs, check_vma=False)
```

profile of v0, /device:TPU:0, one launch (start us, length us, event | category | flops | bytes accessed | tf_op | source)
XLA Modules:
  0.0 245.0 jit_solution(7951676256811415129)
XLA Ops:
  0.6 3.1 %collective-permute-start = (bf16[768,384]{1,0:T(8,128)(2,1)}, bf16[768,384]{1,0:T(8,128)(2,1)}, u32[]{:S(2)}, u32[]{:S(2)}) collective-permute-start(bf16[768,384]{1,0:T(8,128)(2,1)} %out_ref.1), channel_id=1, source_target_pairs={{0,1},{1,0},{2,3},{3,2},{4,5},{5,4},{6,7},{7,6},{8,9},{9,8},{10,11... | collective-permute-start | bytes 1769480 | tf_op jit(solution)/shard_map/ppermute | solution.py:969
  3.7 1.6 compare_select_fusion
  5.4 0.8 fusion.26
  6.2 0.6 fusion.28
  6.8 0.8 fusion.29
  8.2 0.7 pad_add_fusion
  8.9 0.9 fusion.1
  10.5 0.7 broadcast_in_dim.42.query_bias_ref
  11.2 0.7 broadcast_in_dim.43.value_bias_ref
  11.9 0.7 stack.36
  12.6 0.7 stack.37
  13.3 0.7 stack.38
  14.0 0.7 stack.39
  14.6 0.7 stack.40
  15.3 0.7 stack.41
  16.0 0.6 fusion.30
  17.9 0.8 pad.24.memory_ref
  18.7 0.0 copy-start.4
  18.7 1.5 copy-done.4
  20.2 1.1 copy-done.11
  21.3 27.8 %project_window.1 = (bf16[3584,384]{1,0:T(8,128)(2,1)S(1)}, bf16[3584,384]{1,0:T(8,128)(2,1)S(1)}, bf16[3584,384]{1,0:T(8,128)(2,1)S(1)}, bf16[512,768]{1,0:T(8,128)(2,1)S(1)}) custom-call(bf16[512,768]{1,0:T(8,128)(2,1)S(1)} %bitcast.27, s32[8,3584]{1,0:T(8,128)S(1)} %broadcast_in_dim.41.slots_ref, bf16[32,768]{1,0:T(8,128)(2,1)S(1)} %pad.24.memory_ref, ...), custom_call_target="tpu_custom_call" | custom-call | tf_op jit(solution)/shard_map/project_window/pallas_call | solution.py:340
  49.2 0.0 copy-start.6
  49.2 0.9 copy-done.6
  50.0 2.0 broadcast_select_fusion
  52.1 1.4 pad_add_fusion.1.rng_ref
  53.4 6.0 %attention_forward.1 = (bf16[512,384]{1,0:T(8,128)(2,1)S(1)}, f32[512,128]{1,0:T(8,128)S(1)}) custom-call(s32[4]{0:T(128)S(1)} %pad_add_fusion.1.rng_ref, bf16[3584,384]{1,0:T(8,128)(2,1)S(1)} %get-tuple-element.38.q_ref, bf16[3584,384]{1,0:T(8,128)(2,1)S(1)} %get-tuple-element.39.k_ref, bf16[3584,384]{1,0:T(8,128)(2,1)S(1)} %get-tuple-element.40.v_ref, ...), custom_call_target="tpu_custom_call" | custom-call | tf_op jit(solution)/shard_map/attention_forward/pallas_call | solution.py:124
  59.4 0.0 copy-start
  59.4 1.5 copy-done
  61.0 1.6 copy-done.2
  62.6 0.7 copy-done.8
  63.3 0.6 stack.44.vec_ref
  63.9 0.0 collective-permute-done.other_ref
  63.9 56.7 %feed_forward.1 = (bf16[512,768]{1,0:T(8,128)(2,1)}, f32[512,768]{1,0:T(8,128)}, bf16[512,768]{1,0:T(8,128)(2,1)}, bf16[512,384]{1,0:T(8,128)(2,1)}, bf16[2,4,96,1536]{3,2,1,0:T(8,128)(2,1)}, /*index=5*/f32[8,768]{1,0:T(8,128)}) custom-call(bf16[512,384]{1,0:T(8,128)(2,1)} %copy-done.8, bf16[768,384]{1,0:T(8,128)(2,1)} %out_ref.1, ...), custom_call_target="tpu_custom_call" | custom-call | tf_op jit(solution)/shard_map/feed_forward/pallas_call | solution.py:891
  120.7 0.0 copy-start.9
  120.7 2.4 slice_bitcast_fusion
  123.1 1.5 collective-permute-start.1
  124.6 0.1 fusion.refs_7_
  124.7 0.0 copy-done.9
  124.8 0.0 copy-start.10
  124.8 1.1 copy-done.10
  125.9 1.0 copy-done.12
  126.9 22.3 %gather_grads.1 = (bf16[3584,384]{1,0:T(8,128)(2,1)S(1)}, f32[16,3584]{1,0:T(8,128)S(1)}, f32[512,128]{1,0:T(8,128)S(1)}, bf16[768,384]{1,0:T(8,128)(2,1)S(1)}) custom-call(bf16[512,384]{1,0:T(8,128)(2,1)S(1)} %copy-done.12, bf16[512,384]{1,0:T(8,128)(2,1)S(1)} %copy-done.9, f32[512,128]{1,0:T(8,128)S(1)} %get-tuple-element.46.lse_ref, ...), custom_call_target="tpu_custom_call" | custom-call | tf_op jit(solution)/shard_map/gather_grads/pallas_call | solution.py:392
  149.2 0.0 copy-start.1
  149.2 1.8 copy-done.1
  151.0 1.8 copy-done.3
  152.8 13.5 %attention_backward.1.refs_3_ = bf16[512,1152]{1,0:T(8,128)(2,1)S(1)} custom-call(s32[4]{0:T(128)S(1)} %pad_add_fusion.1.rng_ref, bf16[3584,384]{1,0:T(8,128)(2,1)S(1)} %get-tuple-element.38.q_ref, bf16[3584,384]{1,0:T(8,128)(2,1)S(1)} %copy-done.1, bf16[3584,384]{1,0:T(8,128)(2,1)S(1)} %copy-done.3, bf16[3584,384]{1,0:T(8,128)(2,1)S(1)} %get-tuple-element.49.g_ref, ...), custom_call_target="tpu_custom_call" | custom-call | tf_op jit(solution)/shard_map/attention_backward/pallas_call | solution.py:190
  166.3 0.0 copy-start.5
  166.3 1.0 copy-done.5
  167.3 0.0 collective-permute-done.1.refs_1_
  167.3 0.0 copy-done.7
  167.3 0.0 copy-done.13
  167.3 0.0 copy-start.14
  167.3 70.4 %tail.1 = (f32[96,1536]{1,0:T(8,128)S(1)}, f32[96,1536]{1,0:T(8,128)S(1)}, f32[96,384]{1,0:T(8,128)S(1)}, f32[3,96,384]{2,1,0:T(8,128)S(1)}, bf16[512,768]{1,0:T(8,128)(2,1)S(1)}, /*index=5*/f32[4,8,768]{2,1,0:T(8,128)S(1)}) custom-call(bf16[2,4,96,1536]{3,2,1,0:T(8,128)(2,1)} %get-tuple-element.44.refs_0_, ...), custom_call_target="tpu_custom_call" | custom-call | tf_op jit(solution)/shard_map/tail/pallas_call | solution.py:698
  237.7 0.6 slice.193
  238.4 0.6 slice_reduce_fusion
  239.0 0.1 constant_dynamic-slice_fusion
  239.1 0.5 slice_bitcast_fusion.1
  239.6 0.6 reshape.51
  240.2 0.9 copy.39
  241.1 0.9 copy.40
  242.0 0.8 copy.41
  242.7 0.7 copy.42
  243.4 0.8 copy.43
  244.2 0.8 copy.44
  (17 shorter events, 0.1 us)
Async XLA Ops:
  0.6 63.3 %collective-permute-start = (bf16[768,384]{1,0:T(8,128)(2,1)}, bf16[768,384]{1,0:T(8,128)(2,1)}, u32[]{:S(2)}, u32[]{:S(2)}) collective-permute-start(bf16[768,384]{1,0:T(8,128)(2,1)} %out_ref.1), channel_id=1, source_target_pairs={{0,1},{1,0},{2,3},{3,2},{4,5},{5,4},{6,7},{7,6},{8,9},{9,8},{10,11... | collective-permute-start | bytes 1769480 | tf_op jit(solution)/shard_map/ppermute | solution.py:969
  18.7 1.5 copy-start.4
  20.2 1.1 copy-start.11
  49.2 0.9 copy-start.6
  59.4 1.5 copy-start
  61.0 1.6 copy-start.2
  62.5 0.7 copy-start.8
  120.7 4.1 %copy-start.9 = (bf16[512,384]{1,0:T(8,128)(2,1)S(1)}, bf16[512,384]{1,0:T(8,128)(2,1)}, u32[]{:S(2)}) copy-start(bf16[512,384]{1,0:T(8,128)(2,1)} %copy-done.8) | copy-start | bytes 1179652
  123.1 44.2 %collective-permute-start.1 = (bf16[4,96,1536]{2,1,0:T(8,128)(2,1)}, bf16[4,96,1536]{2,1,0:T(8,128)(2,1)}, u32[]{:S(2)}, u32[]{:S(2)}) collective-permute-start(bf16[4,96,1536]{2,1,0:T(8,128)(2,1)} %slice_bitcast_fusion), channel_id=1, source_target_pairs={{0,16},{16,0},{1,17},{17,1},{2,18},{18,2},{3,19},{19,3},{4,20},{20... | collective-permute-start | bytes 3538952 | tf_op jit(solution)/shard_map/ppermute | solution.py:983
  124.8 1.1 copy-start.10
  125.9 1.0 copy-start.12
  149.2 1.8 copy-start.1
  151.0 1.8 copy-start.3
  152.8 14.5 %copy-start.7 = (bf16[512,768]{1,0:T(8,128)(2,1)S(1)}, bf16[512,768]{1,0:T(8,128)(2,1)}, u32[]{:S(2)}) copy-start(bf16[512,768]{1,0:T(8,128)(2,1)} %copy-done.6) | copy-start | bytes 2359300
  152.8 14.5 %copy-start.13 = (f32[8,768]{1,0:T(8,128)S(1)}, f32[8,768]{1,0:T(8,128)}, u32[]{:S(2)}) copy-start(f32[8,768]{1,0:T(8,128)} %get-tuple-element.53.refs_8_) | copy-start | bytes 73732
  166.3 1.0 copy-start.5
  167.3 72.9 %copy-start.14 = (bf16[512,768]{1,0:T(8,128)(2,1)S(1)}, bf16[512,768]{1,0:T(8,128)(2,1)}, u32[]{:S(2)}) copy-start(bf16[512,768]{1,0:T(8,128)(2,1)} %get-tuple-element.43) | copy-start | bytes 2359300
where the time goes:
time: 246 us; the launch traced here: 245 us
  Pallas kernels  197 us (80%)
  local copies, waits for them, and re-layouts  32.7 us (13%)
  other arithmetic  7.63 us (3%)
  starting transfers between devices  4.55 us (2%)
  between operations  3.46 us (1%)
    pallas_call x1, Pallas kernels, tail(): pl.pallas_call(functools.partial(tail_kernel, dps, seqs, width), out_shap...  70.4 us
    pallas_call x1, Pallas kernels, feed_forward(): pl.pallas_call(functools.partial(feed_kernel, dps, seqs, span), out_shape...  56.7 us
    pallas_call x1, Pallas kernels, project_window(): pl.pallas_call(functools.partial(project_kernel, count, parts), out_shape...  27.8 us
    pallas_call x1, Pallas kernels, gather_grads(): pl.pallas_call(functools.partial(grads_kernel, count, parts), out_shape=(...  22.3 us
    unnamed x36, local copies, waits for them, and re-layouts  18.9 us
    pallas_call x1, Pallas kernels, attention_backward(): pl.pallas_call(functools.partial(bwd_kernel, bq, bk, own), out_shape=jax....  13.5 us
    pallas_call x1, Pallas kernels, attention_forward(): pl.pallas_call(functools.partial(fwd_kernel, bq, bk, own), out_shape=(jax...  5.97 us
  transfers between devices with their start and end apart: 2, of which 0 were waited for; matrix products, arithmetic and copies ran while one was open for 7% of the time, Pallas kernels for 28%

commit v1 on v0

--- a/solution.py
+++ b/solution.py
@@ -18,7 +18,7 @@
 NEG = -1e30
 FLOOR = -1e29
 VMEM = pl.BlockSpec(memory_space=pltpu.VMEM)
-SMEM = pl.BlockSpec(memory_space=pltpu.SMEM)
+HBM = pl.BlockSpec(memory_space=pltpu.HBM)
 
 
 def remote(source, target, send_sem, recv_sem, **where):
@@ -59,8 +59,16 @@
         target_ref[2 * pair] = jnp.where(keep, block, jnp.zeros_like(block))
         target_ref[2 * pair + 1] = jnp.where(keep, jnp.zeros_like(block), block)
 
-def sweep(rng_ref, b, body):
-    first, full_first, full_last, last = (rng_ref[4 * b + i] for i in range(4))
+def sweep(ids_ref, start, count, bk, body):
+    mine, every = ids_ref[0:1, pl.ds(start, count)], ids_ref[0:1, :]
+    low, high = jnp.min(mine), jnp.max(mine)
+    begin = jnp.sum(jnp.where(every < low, 1.0, 0.0)).astype(jnp.int32)
+    end = jnp.sum(jnp.where(every <= high, 1.0, 0.0)).astype(jnp.int32)
+    shift = bk.bit_length() - 1
+    first, last = begin >> shift, (end + bk - 1) >> shift
+    full_first, full_last = (begin + bk - 1) >> shift, end >> shift
+    whole = jnp.logical_and(low == high, full_first < full_last)
+    full_first, full_last = jnp.where(whole, full_first, first), jnp.where(whole, full_last, first)
     lax.fori_loop(full_first, full_last, lambda j, c: body(j, False, c), 0)
 
     def edge(i, c):
@@ -69,7 +77,7 @@
 
     lax.fori_loop(0, last - first - (full_last - full_first), edge, 0)
 
-def fwd_kernel(bq, bk, own, rng_ref, q_ref, k_ref, v_ref, ids_ref, o_ref, lse_ref, acc_ref, max_ref, q_heads, cols_ref):
+def fwd_kernel(bq, bk, own, q_ref, k_ref, v_ref, ids_ref, o_ref, lse_ref, acc_ref, max_ref, q_heads, cols_ref):
     pairs = q_ref.shape[1] // 128
     rows = o_ref.shape[0]
     low_q, low_k = low_half((bq, 128)), low_half((bk, 128))
@@ -103,7 +111,7 @@
                 pair_step(pair, carry)
             return carry
 
-        sweep(rng_ref, qb, step)
+        sweep(ids_ref, pl.multiple_of(own + qb * bq, bq), bq, bk, step)
         stats = jnp.zeros((bq, 128), F32)
         lane = lax.broadcasted_iota(jnp.int32, (bq, 128), 1)
         for pair in range(pairs):
@@ -118,20 +126,20 @@
 
     lax.fori_loop(0, rows // bq, block, 0)
 
-def attention_forward(rng, query, key, value, ids, rows, own, bq=256, bk=256):
+def attention_forward(query, key, value, ids, rows, own, bq=256, bk=256):
     width = query.shape[1]
     heads = width // 64
     return pl.pallas_call(
         functools.partial(fwd_kernel, bq, bk, own),
         out_shape=(jax.ShapeDtypeStruct((rows, width), BF16), jax.ShapeDtypeStruct((rows, 128), F32)),
-        in_specs=[pl.BlockSpec(memory_space=pltpu.SMEM)] + [pl.BlockSpec(memory_space=pltpu.VMEM)] * 4,
+        in_specs=[VMEM] * 4,
         out_specs=(pl.BlockSpec(memory_space=pltpu.VMEM),) * 2,
         scratch_shapes=[pltpu.VMEM((heads, bq, 128), F32), pltpu.VMEM((heads, bq, 128), F32), pltpu.VMEM((heads, bq, 128), BF16), pltpu.VMEM((bq, 128), F32)],
         compiler_params=pltpu.CompilerParams(vmem_limit_bytes=24 << 20),
         name="attention_forward",
-    )(rng, query, key, value, ids)
-
-def bwd_kernel(bq, bk, own, rng_ref, q_ref, k_ref, v_ref, g_ref, ids_ref, lse_ref, along_ref, rows_ref, out_ref, dq_acc, dk_acc, dv_acc, q_heads, k_heads, v_heads, g_heads, lse_cols, along_cols, cols_ref):
+    )(query, key, value, ids)
+
+def bwd_kernel(bq, bk, own, q_ref, k_ref, v_ref, g_ref, ids_ref, lse_ref, along_ref, rows_ref, out_ref, dq_acc, dk_acc, dv_acc, q_heads, k_heads, v_heads, g_heads, lse_cols, along_cols, cols_ref):
     rows, width = out_ref.shape[0], q_ref.shape[1]
     pairs = width // 128
     heads = 2 * pairs
@@ -175,7 +183,7 @@
                 pair_step(pair, carry)
             return carry
 
-        sweep(rng_ref, b, step)
+        sweep(ids_ref, pl.multiple_of(own + start, bq), bq, bk, step)
         for which, (acc, factor) in enumerate(((dq_acc, 0.125), (dk_acc, 1.0), (dv_acc, 1.0))):
             for pair in range(pairs):
                 both = jnp.where(low_q, acc[2 * pair], acc[2 * pair + 1]) * factor
@@ -184,18 +192,18 @@
 
     lax.fori_loop(0, rows // bq, block, 0)
 
-def attention_backward(rng, query, key, value, grads, ids, lse, along, stat_rows, rows, own, bq=256, bk=256):
+def attention_backward(query, key, value, grads, ids, lse, along, stat_rows, rows, own, bq=256, bk=256):
     width = query.shape[1]
     heads = width // 64
     return pl.pallas_call(
         functools.partial(bwd_kernel, bq, bk, own),
         out_shape=jax.ShapeDtypeStruct((rows, 3 * width), BF16),
-        in_specs=[pl.BlockSpec(memory_space=pltpu.SMEM)] + [pl.BlockSpec(memory_space=pltpu.VMEM)] * 8,
+        in_specs=[VMEM] * 8,
         out_specs=pl.BlockSpec(memory_space=pltpu.VMEM),
         scratch_shapes=[pltpu.VMEM((heads, bq, 128), F32)] * 3 + [pltpu.VMEM((heads, bq, 128), BF16)] * 4 + [pltpu.VMEM((heads, bq, 128), F32)] * 2 + [pltpu.VMEM((bq, 128), F32)],
         compiler_params=pltpu.CompilerParams(vmem_limit_bytes=40 << 20),
         name="attention_backward",
-    )(rng, query, key, value, grads, ids, lse, along, stat_rows)
+    )(query, key, value, grads, ids, lse, along, stat_rows)
 
 class Halo:
     def __init__(self, count, pieces, send_sem, recv_sem):
@@ -272,7 +280,7 @@
 
 
 def project_kernel(count, parts, own_ref, slots_ref, memory_ref, weight_ref, query_bias_ref, value_bias_ref,
-                   q_ref, k_ref, v_ref, source_ref, window_ref, send_sem, recv_sem):
+                   q_ref, k_ref, v_ref, source_ref, window_ref, weight, send_sem, recv_sem, local_sem):
     block = own_ref.shape[0]
     rows = block // parts
     tile = 256
@@ -285,6 +293,13 @@
     halo.greet()
     for part in range(parts):
         halo.send(part)
+    local = [
+        pltpu.make_async_copy(own_ref, window_ref.at[pl.ds(REACH * block, block)], local_sem.at[0]),
+        pltpu.make_async_copy(weight_ref, weight, local_sem.at[1]),
+    ]
+    for copy in local:
+        copy.start()
+    query_bias, value_bias = query_bias_ref[...].reshape(1, -1), value_bias_ref[...].reshape(1, -1)
 
     def project(load, start, keep):
         hot = (lax.broadcasted_iota(jnp.int32, (32, tile), 0) == slots_ref[0:1, pl.ds(start, tile)]).astype(F32).astype(BF16)
@@ -294,9 +309,9 @@
         source = jnp.where(inside > 0.5, chosen, load().astype(F32)).astype(BF16)
         keep(source)
         out = pl.ds(start, tile)
-        q_ref[out, :] = (dot(source, weight_ref[0]) + query_bias_ref[...]).astype(BF16) * 0.125
-        k_ref[out, :] = dot(source, weight_ref[1]).astype(BF16)
-        v_ref[out, :] = (dot(source, weight_ref[2]) + value_bias_ref[...]).astype(BF16)
+        q_ref[out, :] = (dot(source, weight[0]) + query_bias).astype(BF16) * 0.125
+        k_ref[out, :] = dot(source, weight[1]).astype(BF16)
+        v_ref[out, :] = (dot(source, weight[2]) + value_bias).astype(BF16)
 
     def own_tile(i, carry):
         at = pl.ds(pl.multiple_of(i * tile, tile), tile)
@@ -304,9 +319,12 @@
         def keep(source):
             source_ref[at, :] = source
 
-        project(lambda: own_ref[at, :], pl.multiple_of(REACH * block + i * tile, tile), keep)
+        start = pl.multiple_of(REACH * block + i * tile, tile)
+        project(lambda: window_ref[pl.ds(start, tile), :], start, keep)
         return carry
 
+    for copy in local:
+        copy.wait()
     lax.fori_loop(0, tiles, own_tile, 0)
     for part in range(parts):
         halo.relay(part)
@@ -340,12 +358,14 @@
     return pl.pallas_call(
         functools.partial(project_kernel, count, parts),
         out_shape=(wide_out, wide_out, wide_out, jax.ShapeDtypeStruct((rows, dim), BF16)),
-        in_specs=[VMEM] * 6,
+        in_specs=[HBM, VMEM, VMEM, HBM, VMEM, VMEM],
         out_specs=(VMEM,) * 4,
         scratch_shapes=[
             pltpu.VMEM((total, dim), BF16),
+            pltpu.VMEM(weight.shape, BF16),
             pltpu.SemaphoreType.DMA((7, parts)),
             pltpu.SemaphoreType.DMA((7, parts)),
+            pltpu.SemaphoreType.DMA((2,)),
         ],
         compiler_params=pltpu.CompilerParams(collective_id=collective_id, has_side_effects=True, vmem_limit_bytes=40 << 20),
         name="project_window",
@@ -479,7 +499,7 @@
     def start_early(c):
         lanes = slice(c * width, c * width + width)
         for j in range(zs):
-            total = early_refs[0][0, j, :, lanes].astype(F32)
+            total = early_refs[0][j, :, lanes].astype(F32)
             for k in range(1, dps):
                 total = total + early_refs[k][j, :, lanes].astype(F32)
             mine[c, j] = total.astype(BF16)
@@ -683,15 +703,15 @@
 def tail(early, out, proj, source, weight, input1, select, small, dps, seqs):
     zs = seqs // 2
     dim = source.shape[1]
-    hidden = early[0].shape[3] * dps // 2
+    hidden = early[0].shape[2] * dps // 2
     rows = proj.shape[0]
     block = dim // seqs
     mixed = out.shape[1] + proj.shape[1]
     late = 2
     chunk = mixed // late
     width = -(-chunk // (128 * dps)) * 128
-    width = early[0].shape[3] if early[0].shape[3] % width else width
-    chunks = early[0].shape[3] // width + late
+    width = early[0].shape[2] if early[0].shape[2] % width else width
+    chunks = early[0].shape[2] // width + late
     steps = 4
     table = (OWNERS,) + small.shape
     dma = pltpu.SemaphoreType.DMA
@@ -734,9 +754,15 @@
     )(*early, out, proj, source, weight, input1, select, small)
 
 
-def feed_kernel(dps, seqs, span, mixed_ref, out_ref, other_ref, source_ref, up_ref, down_ref, vec_ref, grad_ref,
-                y_ref, input1_ref, low_ref, mixed_grad_ref, shares_ref, small_ref,
-                out_all, mixed_all, first_ref, hat_ref, scale_ref, first_low, act_ref, slope_ref, second_ref, down_grad, up_grad,
+def feed_kernel(dps, seqs, span, *refs):
+    (mixed_ref, out_ref, other_ref, source_ref, up_hbm, down_hbm, grad_ref), vectors = refs[:7], refs[7:14]
+    share_refs = refs[14:14 + dps]
+    feed_body(dps, seqs, span, mixed_ref, out_ref, other_ref, source_ref, up_hbm, down_hbm, grad_ref, vectors, share_refs, *refs[14 + dps:])
+
+
+def feed_body(dps, seqs, span, mixed_ref, out_ref, other_ref, source_ref, up_hbm, down_hbm, grad_ref, vectors, share_refs,
+                y_ref, input1_ref, low_ref, mixed_grad_ref, small_ref,
+                up_ref, down_ref, w_sems, out_all, mixed_all, first_ref, hat_ref, scale_ref, first_low, act_ref, slope_ref, second_ref, down_grad, up_grad,
                 y_send, y_recv, z_send, z_recv, grads, a_recv, m_sems, y_sems, z_sems, a_sems):
     rows, dim = source_ref.shape
     width, hidden = mixed_ref.shape[1], up_ref.shape[1]
@@ -783,14 +809,19 @@
     def add_rows(row, x):
         small_ref[row:row + 1, :] += jnp.sum(x, axis=0, keepdims=True)
 
-    out_bias, gain1, shift1, down_bias, gain2, shift2 = (vec_ref[i:i + 1, :] for i in range(6))
+    out_bias, gain1, shift1, down_bias, gain2, shift2, up_bias = (ref[...].reshape(1, -1) for ref in vectors)
 
     for i in range(spans):
         m_copy(i).start()
+    loads = [pltpu.make_async_copy(up_hbm, up_ref, w_sems.at[0]), pltpu.make_async_copy(down_hbm, down_ref, w_sems.at[1])]
+    for copy in loads:
+        copy.start()
     out_all[:, mine] = out_ref[...]
     out_all[:, theirs] = other_ref[...]
     mixed_all[:, mine] = mixed_ref[...]
     small_ref[...] = jnp.zeros_like(small_ref)
+    for copy in loads:
+        copy.wait()
 
     def forward(i, carry):
         m_copy(i).wait()
@@ -805,7 +836,7 @@
         part = jnp.zeros((span, dim), F32)
         for k in range(2):
             cols = slice(k * dim, (k + 1) * dim)
-            up = dot(low, up_ref[:, cols]) + vec_ref[6 + k:7 + k, :]
+            up = dot(low, up_ref[:, cols]) + up_bias[:, cols]
             below = 0.5 + 0.5 * lax.erf(up * 0.7071067811865476)
             act = (up * below).astype(BF16)
             slope_ref[at(i), cols] = below + up * jnp.exp(-0.5 * up * up) * 0.3989422804014327
@@ -879,7 +910,11 @@
                     first, last = max(p * share, which * hidden), min((p + 1) * share, (which + 1) * hidden)
                     cols = slice(first - which * hidden, last - which * hidden)
                     total = grads[which, own, cols].astype(F32) + a_recv[which, j, :, cols].astype(F32)
-                    shares_ref[lax.rem(p - d + dps, dps), j, :, first - p * share:last - p * share] = total.astype(BF16)
+                    for k in range(dps):
+
+                        @pl.when(lax.rem(p - d + dps, dps) == k)
+                        def _():
+                            share_refs[k][j, :, first - p * share:last - p * share] = total.astype(BF16)
 
 
 def feed_forward(mixed, out_weight, out_other, source, up, down, vectors, grad, dps, seqs, span=256):
@@ -890,17 +925,19 @@
     dma = pltpu.SemaphoreType.DMA
     return pl.pallas_call(
         functools.partial(feed_kernel, dps, seqs, span),
-        out_shape=(
+        out_shape=(jax.ShapeDtypeStruct((zs, block, 2 * hidden // dps), BF16),) * dps + (
             jax.ShapeDtypeStruct((rows, dim), BF16),
             jax.ShapeDtypeStruct((rows, dim), F32),
             jax.ShapeDtypeStruct((rows, dim), BF16),
             jax.ShapeDtypeStruct((rows, width), BF16),
-            jax.ShapeDtypeStruct((dps, zs, block, 2 * hidden // dps), BF16),
             jax.ShapeDtypeStruct((8, dim), F32),
         ),
-        in_specs=[VMEM] * 8,
-        out_specs=(VMEM,) * 6,
+        in_specs=[VMEM] * 4 + [HBM] * 2 + [VMEM] * 8,
+        out_specs=(VMEM,) * (dps + 5),
         scratch_shapes=[
+            pltpu.VMEM((dim, hidden), BF16),
+            pltpu.VMEM((dim, hidden), BF16),
+            dma((2,)),
             pltpu.VMEM((dim, 2 * width), BF16),
             pltpu.VMEM((rows, 2 * width), BF16),
             pltpu.VMEM((rows, dim), F32),
@@ -925,7 +962,7 @@
         ],
         compiler_params=pltpu.CompilerParams(collective_id=3, has_side_effects=True, vmem_limit_bytes=56 << 20),
         name="feed_forward",
-    )(mixed, out_weight, out_other, source, up, down, vectors, grad)
+    )(mixed, out_weight, out_other, source, up, down, grad, *vectors)
 
 
 def memory_slots(id_row):
@@ -935,17 +972,6 @@
     before = sum((padded[READ_ROWS - k:READ_ROWS - k + count] == id_row).astype(jnp.int32) for k in range(1, READ_ROWS + 1))
     behind = sum((padded[READ_ROWS + k:READ_ROWS + k + count] == id_row).astype(jnp.int32) for k in range(1, READ_ROWS + 1))
     return jnp.where(before < READ_ROWS, before, jnp.where(behind < READ_ROWS, 2 * READ_ROWS - 1 - behind, -1))
-
-
-def document_blocks(id_row, own_ids, window_start, bk):
-    bounds = jnp.stack([own_ids[0], own_ids[-1] + 1])
-    start_end = jnp.sum((id_row[None, :] < bounds[:, None]).astype(jnp.int32), axis=1) - window_start
-    shift = bk.bit_length() - 1
-    floor, ceil = start_end >> shift, (start_end + bk - 1) >> shift
-    first, last = floor[0], ceil[1]
-    whole = jnp.logical_and(bounds[0] + 1 == bounds[1], ceil[0] < floor[1])
-    inside = jnp.where(whole, jnp.stack([ceil[0], floor[1]]), first)
-    return jnp.concatenate([floor[:1], inside, ceil[1:]]).astype(jnp.int32)
 
 
 def on_device(dps, seqs, tokens, doc_ids, memory, qkv_weight, query_bias, value_bias, out_weight, out_bias, norm1_gain, norm1_bias, up_weight, up_bias, down_weight, down_bias, norm2_gain, norm2_bias, out_grad):
@@ -958,12 +984,9 @@
     s = lax.axis_index("seq")
     id_row = doc_ids[0]
     edge = jnp.full((own,), -1, jnp.int32)
-    window_start = s * rows - own
     slots = memory_slots(id_row)
     window_slots = lax.dynamic_slice_in_dim(jnp.concatenate([edge, slots, edge]), s * rows, pieces * rows, 0)
-    window_ids = lax.dynamic_slice_in_dim(jnp.concatenate([edge, id_row, edge]), s * rows, pieces * rows, 0)
-    own_ids = window_ids[own:own + rows]
-    blocks = document_blocks(id_row, own_ids, window_start, bk)
+    window_ids = lax.dynamic_slice_in_dim(jnp.concatenate([edge, id_row, jnp.full((own,), 1 << 20, jnp.int32)]), s * rows, pieces * rows, 0)
     ids = jnp.broadcast_to(window_ids.astype(F32)[None], (8, pieces * rows))
 
     out_other = lax.ppermute(out_weight, "tensor", [(0, 1), (1, 0)])
@@ -971,18 +994,18 @@
     slots_row = jnp.broadcast_to(window_slots[None], (8, pieces * rows))
     memory_pad = jnp.pad(memory, ((0, 32 - memory.shape[0]), (0, 0)))
     query, key, value, source = project_window(
-        tokens[0], slots_row, memory_pad, weight, query_bias[None], value_bias[None], seqs, 1)
+        tokens[0], slots_row, memory_pad, weight, query_bias, value_bias, seqs, 1)
     own_slots = window_slots[own:own + rows]
 
-    mixed_low, logsums = attention_forward(blocks, query, key, value, ids, rows, own, bq, bk)
-
-    vectors = jnp.stack([out_bias, norm1_gain, norm1_bias, down_bias, norm2_gain, norm2_bias, up_bias[:2 * width], up_bias[2 * width:]])
-    output, grad_input1, branch_grad, mixed_grad, shares, small = feed_forward(
+    mixed_low, logsums = attention_forward(query, key, value, ids, rows, own, bq, bk)
+
+    vectors = (out_bias, norm1_gain, norm1_bias, down_bias, norm2_gain, norm2_bias, up_bias)
+    *shares, output, grad_input1, branch_grad, mixed_grad, small = feed_forward(
         mixed_low, out_weight, out_other, source, up_weight, down_weight, vectors, out_grad[0], dps, seqs)
-    early = [shares] + [
+    early = shares[:1] + [
         lax.ppermute(shares[k], "dp", [(i, (i + k) % dps) for i in range(dps)]) for k in range(1, dps)]
     grads_window, stats_window, along_cols, grad_out_weight = gather_grads(mixed_grad, mixed_low, logsums, branch_grad, seqs, 2)
-    proj_grad = attention_backward(blocks, query, key, value, grads_window, ids, logsums, along_cols, stats_window, rows, own, bq, bk)
+    proj_grad = attention_backward(query, key, value, grads_window, ids, logsums, along_cols, stats_window, rows, own, bq, bk)
 
     select = (own_slots[:, None] == jnp.arange(32, dtype=jnp.int32)[None, :]).astype(BF16)
     up_sum, down_sum, out_sum, qkv_sum, input_grad, small = tail(

time: 246 us -> 221 us (0.90)
  local copies, waits for them, and re-layouts: 32.7 us -> 19.5 us
  other arithmetic: 7.63 us -> 2.59 us
  Pallas kernels: 197 us -> 193 us
  between operations: 3.46 us -> 0.88 us
    another operation x9 -> x0, local copies, waits for them, and re-layouts: 4.79 us -> none  [on_device(): jnp.stack([out_bias, norm1_gain, norm1_bias, down_bias, norm2_gain, norm2...]
    unnamed x36 -> x42, local copies, waits for them, and re-layouts: 18.9 us -> 16.2 us
  transfers between devices with their start and end apart: 2 -> 2, of which waited for: 0 -> 0; matrix products, arithmetic and copies ran while one was open for 7% -> 2% of each run, Pallas kernels for 28% -> 30%
where the time goes in v1:
time: 221 us
  Pallas kernels  193 us (87%)
  local copies, waits for them, and re-layouts  19.5 us (9%)
  starting transfers between devices  4.62 us (2%)
  other arithmetic  2.59 us (1%)
    pallas_call x1, Pallas kernels, tail(): pl.pallas_call(functools.partial(tail_kernel, dps, seqs, width), out_shap...  69.8 us
    pallas_call x1, Pallas kernels, feed_forward(): pl.pallas_call(functools.partial(feed_kernel, dps, seqs, span), out_shape...  56 us
    pallas_call x1, Pallas kernels, project_window(): pl.pallas_call(functools.partial(project_kernel, count, parts), out_shape...  27.8 us
    pallas_call x1, Pallas kernels, gather_grads(): pl.pallas_call(functools.partial(grads_kernel, count, parts), out_shape=(...  20.8 us
    unnamed x42, local copies, waits for them, and re-layouts  16.2 us
    pallas_call x1, Pallas kernels, attention_backward(): pl.pallas_call(functools.partial(bwd_kernel, bq, bk, own), out_shape=jax....  12.8 us
    pallas_call x1, Pallas kernels, attention_forward(): pl.pallas_call(functools.partial(fwd_kernel, bq, bk, own), out_shape=(jax...  5.58 us
  transfers between devices with their start and end apart: 2, of which 0 were waited for; matrix products, arithmetic and copies ran while one was open for 2% of the time, Pallas kernels for 30%

profile of v1, /device:TPU:0, one launch (start us, length us, event | category | flops | bytes accessed | tf_op | source)
XLA Modules:
  0.0 220.5 jit_solution(15207514656058930232)
XLA Ops:
  0.6 3.1 %collective-permute-start = (bf16[768,384]{1,0:T(8,128)(2,1)}, bf16[768,384]{1,0:T(8,128)(2,1)}, u32[]{:S(2)}, u32[]{:S(2)}) collective-permute-start(bf16[768,384]{1,0:T(8,128)(2,1)} %refs_1_.1), channel_id=1, source_target_pairs={{0,1},{1,0},{2,3},{3,2},{4,5},{5,4},{6,7},{7,6},{8,9},{9,8},{10,11... | collective-permute-start | bytes 1769480 | tf_op jit(solution)/shard_map/ppermute | solution.py:992
  3.7 0.8 pad.24.memory_ref
  4.5 1.6 compare_select_fusion
  6.1 0.8 fusion.5
  7.0 0.0 copy-start.4
  7.0 1.5 copy-done.4
  8.5 0.0 copy-start.12
  8.5 1.1 copy-done.12
  9.6 0.0 copy-start.15
  9.6 0.7 copy-done.15
  10.3 0.0 copy-start.16
  10.3 0.7 copy-done.16
  11.0 27.8 %project_window.1 = (bf16[3584,384]{1,0:T(8,128)(2,1)S(1)}, bf16[3584,384]{1,0:T(8,128)(2,1)S(1)}, bf16[3584,384]{1,0:T(8,128)(2,1)S(1)}, bf16[512,768]{1,0:T(8,128)(2,1)S(1)}) custom-call(bf16[512,768]{1,0:T(8,128)(2,1)S(1)} %bitcast.23, s32[8,3584]{1,0:T(8,128)S(1)} %broadcast_in_dim.32.slots_ref, bf16[32,768]{1,0:T(8,128)(2,1)S(1)} %pad.24.memory_ref, ...), custom_call_target="tpu_custom_call" | custom-call | tf_op jit(solution)/shard_map/project_window/pallas_call | solution.py:358
  38.8 0.0 copy-start
  38.8 0.0 copy-start.2
  38.8 0.0 copy-start.6
  38.8 5.6 %attention_forward.1 = (bf16[512,384]{1,0:T(8,128)(2,1)S(1)}, f32[512,128]{1,0:T(8,128)S(1)}) custom-call(bf16[3584,384]{1,0:T(8,128)(2,1)S(1)} %get-tuple-element.39.q_ref, bf16[3584,384]{1,0:T(8,128)(2,1)S(1)} %get-tuple-element.40.k_ref, bf16[3584,384]{1,0:T(8,128)(2,1)S(1)} %get-tuple-element.41.v_ref, f32[8,3584]{1,0:T(8,128)S(1)} %broadcast_in_dim.34.ids_ref), custom_call_target="tpu_custom_call" | custom-call | tf_op jit(solution)/shard_map/attention_forward/pallas_call | solution.py:132
  44.4 0.0 copy-done
  44.4 0.0 copy-done.2
  44.4 0.0 copy-done.6
  44.5 0.0 copy-start.8
  44.5 0.7 copy-done.8
  45.2 0.0 collective-permute-done.refs_2_
  45.2 0.0 copy-start.9
  45.2 56.0 %feed_forward.1 = (bf16[4,96,1536]{2,1,0:T(8,128)(2,1)}, bf16[4,96,1536]{2,1,0:T(8,128)(2,1)}, bf16[512,768]{1,0:T(8,128)(2,1)}, f32[512,768]{1,0:T(8,128)}, bf1...) custom-call(bf16[512,384]{1,0:T(8,128)(2,1)} %copy-done.8, bf16[768,384]{1,0:T(8,128)(2,1)} %refs_1_.1, ...), custom_call_target="tpu_custom_call" | custom-call | tf_op jit(solution)/shard_map/feed_forward/pallas_call | solution.py:926
  101.2 1.6 collective-permute-start.1
  102.8 0.1 fusion.refs_7_
  102.9 0.0 copy-done.9
  103.0 0.0 copy-start.11
  103.0 1.1 copy-done.11
  104.1 0.0 copy-start.13
  104.1 1.0 copy-done.13
  105.1 20.8 %gather_grads.1 = (bf16[3584,384]{1,0:T(8,128)(2,1)S(1)}, f32[16,3584]{1,0:T(8,128)S(1)}, f32[512,128]{1,0:T(8,128)S(1)}, bf16[768,384]{1,0:T(8,128)(2,1)S(1)}) custom-call(bf16[512,384]{1,0:T(8,128)(2,1)S(1)} %copy-done.13, bf16[512,384]{1,0:T(8,128)(2,1)S(1)} %copy-done.9, f32[512,128]{1,0:T(8,128)S(1)} %get-tuple-element.48.lse_ref, ...), custom_call_target="tpu_custom_call" | custom-call | tf_op jit(solution)/shard_map/gather_grads/pallas_call | solution.py:412
  125.9 0.0 copy-start.1
  125.9 1.8 copy-done.1
  127.7 0.0 copy-start.3
  127.7 1.8 copy-done.3
  129.5 0.0 copy-start.7
  129.5 0.0 copy-start.10
  129.5 0.0 copy-start.14
  129.5 12.8 %attention_backward.1.refs_3_ = bf16[512,1152]{1,0:T(8,128)(2,1)S(1)} custom-call(bf16[3584,384]{1,0:T(8,128)(2,1)S(1)} %get-tuple-element.39.q_ref, bf16[3584,384]{1,0:T(8,128)(2,1)S(1)} %copy-done.1, bf16[3584,384]{1,0:T(8,128)(2,1)S(1)} %copy-done.3, bf16[3584,384]{1,0:T(8,128)(2,1)S(1)} %get-tuple-element.51.g_ref, ...), custom_call_target="tpu_custom_call" | custom-call | tf_op jit(solution)/shard_map/attention_backward/pallas_call | solution.py:198
  142.3 0.0 copy-start.5
  142.3 1.0 copy-done.5
  143.4 0.0 collective-permute-done.1.refs_1_
  143.4 0.0 copy-done.7
  143.4 0.0 copy-done.10
  143.4 0.0 copy-done.14
  143.4 0.0 copy-start.17
  143.4 69.8 %tail.1 = (f32[96,1536]{1,0:T(8,128)S(1)}, f32[96,1536]{1,0:T(8,128)S(1)}, f32[96,384]{1,0:T(8,128)S(1)}, f32[3,96,384]{2,1,0:T(8,128)S(1)}, bf16[512,768]{1,0:T(8,128)(2,1)S(1)}, /*index=5*/f32[4,8,768]{2,1,0:T(8,128)S(1)}) custom-call(bf16[4,96,1536]{2,1,0:T(8,128)(2,1)S(1)} %copy-done.10, bf16[4,96,1536]{2,1,0:T(8,128)(2,1)} %collective-permute-done.1.refs_1_, ...), custom_call_target="tpu_custom_call" | custom-call | tf_op jit(solution)/shard_map/tail/pallas_call | solution.py:718
  213.2 0.6 slice.149
  213.9 0.6 slice_reduce_fusion
  214.5 0.1 constant_dynamic-slice_fusion
  214.5 0.5 slice_bitcast_fusion
  215.1 0.6 reshape.42
  215.7 0.0 copy-done.17
  215.7 0.9 copy.39
  216.6 0.9 copy.40
  217.4 0.8 copy.41
  218.2 0.7 copy.42
  218.9 0.8 copy.43
  219.7 0.8 copy.44
  (7 shorter events, 0.0 us)
Async XLA Ops:
  0.6 44.6 %collective-permute-start = (bf16[768,384]{1,0:T(8,128)(2,1)}, bf16[768,384]{1,0:T(8,128)(2,1)}, u32[]{:S(2)}, u32[]{:S(2)}) collective-permute-start(bf16[768,384]{1,0:T(8,128)(2,1)} %refs_1_.1), channel_id=1, source_target_pairs={{0,1},{1,0},{2,3},{3,2},{4,5},{5,4},{6,7},{7,6},{8,9},{9,8},{10,11... | collective-permute-start | bytes 1769480 | tf_op jit(solution)/shard_map/ppermute | solution.py:992
  7.0 1.5 copy-start.4
  8.5 1.1 copy-start.12
  9.6 0.7 copy-start.15
  10.3 0.7 copy-start.16
  38.8 5.6 %copy-start = (bf16[3584,384]{1,0:T(8,128)(2,1)}, bf16[3584,384]{1,0:T(8,128)(2,1)S(1)}, u32[]{:S(2)}) copy-start(bf16[3584,384]{1,0:T(8,128)(2,1)S(1)} %get-tuple-element.40.k_ref) | copy-start | bytes 8257540
  38.8 5.6 %copy-start.2 = (bf16[3584,384]{1,0:T(8,128)(2,1)}, bf16[3584,384]{1,0:T(8,128)(2,1)S(1)}, u32[]{:S(2)}) copy-start(bf16[3584,384]{1,0:T(8,128)(2,1)S(1)} %get-tuple-element.41.v_ref) | copy-start | bytes 8257540
  38.8 5.6 %copy-start.6 = (bf16[512,768]{1,0:T(8,128)(2,1)}, bf16[512,768]{1,0:T(8,128)(2,1)S(1)}, u32[]{:S(2)}) copy-start(bf16[512,768]{1,0:T(8,128)(2,1)S(1)} %get-tuple-element.43.refs_3_.refs_4_) | copy-start | bytes 2359300
  44.5 0.7 copy-start.8
  45.2 57.7 %copy-start.9 = (bf16[512,384]{1,0:T(8,128)(2,1)S(1)}, bf16[512,384]{1,0:T(8,128)(2,1)}, u32[]{:S(2)}) copy-start(bf16[512,384]{1,0:T(8,128)(2,1)} %copy-done.8) | copy-start | bytes 1179652
  101.2 42.1 %collective-permute-start.1 = (bf16[4,96,1536]{2,1,0:T(8,128)(2,1)}, bf16[4,96,1536]{2,1,0:T(8,128)(2,1)}, u32[]{:S(2)}, u32[]{:S(2)}) collective-permute-start(bf16[4,96,1536]{2,1,0:T(8,128)(2,1)} %get-tuple-element.46), channel_id=1, source_target_pairs={{0,16},{16,0},{1,17},{17,1},{2,18},{18,2},{3,19},{19,3},{4,20},{20... | collective-permute-start | bytes 3538952 | tf_op jit(solution)/shard_map/ppermute | solution.py:1006
  103.0 1.1 copy-start.11
  104.1 1.0 copy-start.13
  125.9 1.8 copy-start.1
  127.7 1.8 copy-start.3
  129.5 13.9 %copy-start.7 = (bf16[512,768]{1,0:T(8,128)(2,1)S(1)}, bf16[512,768]{1,0:T(8,128)(2,1)}, u32[]{:S(2)}) copy-start(bf16[512,768]{1,0:T(8,128)(2,1)} %copy-done.6) | copy-start | bytes 2359300
  129.5 13.9 %copy-start.10 = (bf16[4,96,1536]{2,1,0:T(8,128)(2,1)S(1)}, bf16[4,96,1536]{2,1,0:T(8,128)(2,1)}, u32[]{:S(2)}) copy-start(bf16[4,96,1536]{2,1,0:T(8,128)(2,1)} %get-tuple-element.45.refs_0_) | copy-start | bytes 3538948
  129.5 13.9 %copy-start.14 = (f32[8,768]{1,0:T(8,128)S(1)}, f32[8,768]{1,0:T(8,128)}, u32[]{:S(2)}) copy-start(f32[8,768]{1,0:T(8,128)} %get-tuple-element.55.refs_8_) | copy-start | bytes 73732
  142.3 1.0 copy-start.5
  143.4 72.3 %copy-start.17 = (bf16[512,768]{1,0:T(8,128)(2,1)S(1)}, bf16[512,768]{1,0:T(8,128)(2,1)}, u32[]{:S(2)}) copy-start(bf16[512,768]{1,0:T(8,128)(2,1)} %get-tuple-element.44) | copy-start | bytes 2359300

commit v2 on v1

--- a/solution.py
+++ b/solution.py
@@ -59,7 +59,7 @@
         target_ref[2 * pair] = jnp.where(keep, block, jnp.zeros_like(block))
         target_ref[2 * pair + 1] = jnp.where(keep, jnp.zeros_like(block), block)
 
-def sweep(ids_ref, start, count, bk, body):
+def document_range(ids_ref, start, count, bk):
     mine, every = ids_ref[0:1, pl.ds(start, count)], ids_ref[0:1, :]
     low, high = jnp.min(mine), jnp.max(mine)
     begin = jnp.sum(jnp.where(every < low, 1.0, 0.0)).astype(jnp.int32)
@@ -68,7 +68,11 @@
     first, last = begin >> shift, (end + bk - 1) >> shift
     full_first, full_last = (begin + bk - 1) >> shift, end >> shift
     whole = jnp.logical_and(low == high, full_first < full_last)
-    full_first, full_last = jnp.where(whole, full_first, first), jnp.where(whole, full_last, first)
+    return first, jnp.where(whole, full_first, first), jnp.where(whole, full_last, first), last
+
+
+def sweep(span, body):
+    first, full_first, full_last, last = span
     lax.fori_loop(full_first, full_last, lambda j, c: body(j, False, c), 0)
 
     def edge(i, c):
@@ -111,7 +115,7 @@
                 pair_step(pair, carry)
             return carry
 
-        sweep(ids_ref, pl.multiple_of(own + qb * bq, bq), bq, bk, step)
+        sweep(document_range(ids_ref, pl.multiple_of(own + qb * bq, bq), bq, bk), step)
         stats = jnp.zeros((bq, 128), F32)
         lane = lax.broadcasted_iota(jnp.int32, (bq, 128), 1)
         for pair in range(pairs):
@@ -139,69 +143,92 @@
         name="attention_forward",
     )(query, key, value, ids)
 
-def bwd_kernel(bq, bk, own, q_ref, k_ref, v_ref, g_ref, ids_ref, lse_ref, along_ref, rows_ref, out_ref, dq_acc, dk_acc, dv_acc, q_heads, k_heads, v_heads, g_heads, lse_cols, along_cols, cols_ref):
-    rows, width = out_ref.shape[0], q_ref.shape[1]
+def bwd_kernel(bk, own, q_hbm, k_hbm, v_hbm, g_hbm, ids_ref, lse_ref, along_ref, rows_ref, out_ref, q_ref, k_ref, v_ref, g_ref, sems, dq_acc, dk_acc, dv_acc, q_heads, k_heads, v_heads, g_heads, lse_cols, along_cols, cols_ref):
+    bq, width = out_ref.shape[0], q_ref.shape[1]
     pairs = width // 128
     heads = 2 * pairs
     low_q = low_half((bq, 128))
 
-    def block(b, carry):
-        start = pl.multiple_of(b * bq, bq)
-        mine = pl.ds(start, bq)
-        here = pl.ds(pl.multiple_of(own + start, bq), bq)
-        cols_ref[...] = id_columns(ids_ref, pl.multiple_of(own + start, bq), bq)
-        for source, target in ((q_ref, q_heads), (k_ref, k_heads), (v_ref, v_heads), (g_ref, g_heads)):
-            split_heads(source, here, target, pairs, low_q)
-        for head in range(heads):
-            lse_cols[head] = jnp.broadcast_to(lse_ref[mine, head:head + 1], (bq, 128))
-            along_cols[head] = jnp.broadcast_to(along_ref[mine, head:head + 1], (bq, 128))
-        for acc in (dq_acc, dk_acc, dv_acc):
-            acc[...] = jnp.zeros_like(acc)
-
-        def step(j, masked, carry):
-            there = pl.ds(pl.multiple_of(j * bk, bk), bk)
-            def pair_step(pair, carry):
-                lanes = pl.ds(pair * 128, 128)
-                q_far, k_far, v_far, g_far = (r[there, lanes] for r in (q_ref, k_ref, v_ref, g_ref))
-                def hide(x):
-                    return jnp.where(wide(cols_ref[...], bk) == ids_ref[0:1, there], x, 0.0) if masked else x
-                for odd in range(2):
-                    head = 2 * pair + odd
-                    scores = dot(q_heads[head], k_far, NT)
-                    probs = hide(jnp.exp(scores - wide(lse_cols[head], bk)))
-                    slope = dot(g_heads[head], v_far, NT)
-                    grad = (probs * (slope - wide(along_cols[head], bk))).astype(BF16)
-                    dq_acc[head] += dot(grad, k_far)
-                    scores = dot(k_heads[head], q_far, NT)
-                    probs = hide(jnp.exp(scores - rows_ref[pl.ds(head, 1), there]))
-                    slope = dot(v_heads[head], g_far, NT)
-                    grad = (probs * (slope - rows_ref[pl.ds(8 + head, 1), there])).astype(BF16)
-                    dv_acc[head] += dot(probs.astype(BF16), g_far)
-                    dk_acc[head] += dot(grad, q_far)
-                return carry
-            for pair in range(pairs):
-                pair_step(pair, carry)
+    blocks = document_range(ids_ref, own, bq, bk)
+    first_own, last_own = own // bk, (own + bq) // bk
+
+    def copies(j):
+        there = pl.ds(pl.multiple_of(j * bk, bk), bk)
+        pairs_of = ((q_hbm, q_ref), (k_hbm, k_ref), (v_hbm, v_ref), (g_hbm, g_ref))
+        return [pltpu.make_async_copy(source.at[there], target.at[there], sems.at[i, j]) for i, (source, target) in enumerate(pairs_of)]
+
+    def start_all(j, carry):
+        @pl.when(jnp.logical_or(j < first_own, j >= last_own))
+        def _():
+            for copy in copies(j):
+                copy.start()
+
+        return carry
+
+    for j in range(first_own, last_own):
+        for copy in copies(j):
+            copy.start()
+    lax.fori_loop(blocks[0], blocks[3], start_all, 0)
+    mine, here = pl.ds(0, bq), pl.ds(own, bq)
+    cols_ref[...] = id_columns(ids_ref, own, bq)
+    for acc in (dq_acc, dk_acc, dv_acc):
+        acc[...] = jnp.zeros_like(acc)
+    for head in range(heads):
+        lse_cols[head] = jnp.broadcast_to(lse_ref[mine, head:head + 1], (bq, 128))
+        along_cols[head] = jnp.broadcast_to(along_ref[mine, head:head + 1], (bq, 128))
+    for j in range(first_own, last_own):
+        for copy in copies(j):
+            copy.wait()
+    for source, target in ((q_ref, q_heads), (k_ref, k_heads), (v_ref, v_heads), (g_ref, g_heads)):
+        split_heads(source, here, target, pairs, low_q)
+
+    def step(j, masked, carry):
+        there = pl.ds(pl.multiple_of(j * bk, bk), bk)
+
+        @pl.when(jnp.logical_or(j < first_own, j >= last_own))
+        def _():
+            for copy in copies(j):
+                copy.wait()
+
+        def pair_step(pair, carry):
+            lanes = pl.ds(pair * 128, 128)
+            q_far, k_far, v_far, g_far = (r[there, lanes] for r in (q_ref, k_ref, v_ref, g_ref))
+            def hide(x):
+                return jnp.where(wide(cols_ref[...], bk) == ids_ref[0:1, there], x, 0.0) if masked else x
+            for odd in range(2):
+                head = 2 * pair + odd
+                scores = dot(q_heads[head], k_far, NT)
+                probs = hide(jnp.exp(scores - wide(lse_cols[head], bk)))
+                slope = dot(g_heads[head], v_far, NT)
+                grad = (probs * (slope - wide(along_cols[head], bk))).astype(BF16)
+                dq_acc[head] += dot(grad, k_far)
+                scores = dot(k_heads[head], q_far, NT)
+                probs = hide(jnp.exp(scores - rows_ref[pl.ds(head, 1), there]))
+                slope = dot(v_heads[head], g_far, NT)
+                grad = (probs * (slope - rows_ref[pl.ds(8 + head, 1), there])).astype(BF16)
+                dv_acc[head] += dot(probs.astype(BF16), g_far)
+                dk_acc[head] += dot(grad, q_far)
             return carry
-
-        sweep(ids_ref, pl.multiple_of(own + start, bq), bq, bk, step)
-        for which, (acc, factor) in enumerate(((dq_acc, 0.125), (dk_acc, 1.0), (dv_acc, 1.0))):
-            for pair in range(pairs):
-                both = jnp.where(low_q, acc[2 * pair], acc[2 * pair + 1]) * factor
-                out_ref[mine, which * width + pair * 128:which * width + pair * 128 + 128] = both.astype(BF16)
+        for pair in range(pairs):
+            pair_step(pair, carry)
         return carry
 
-    lax.fori_loop(0, rows // bq, block, 0)
-
-def attention_backward(query, key, value, grads, ids, lse, along, stat_rows, rows, own, bq=256, bk=256):
+    sweep(blocks, step)
+    for which, (acc, factor) in enumerate(((dq_acc, 0.125), (dk_acc, 1.0), (dv_acc, 1.0))):
+        for pair in range(pairs):
+            both = jnp.where(low_q, acc[2 * pair], acc[2 * pair + 1]) * factor
+            out_ref[mine, which * width + pair * 128:which * width + pair * 128 + 128] = both.astype(BF16)
+
+def attention_backward(query, key, value, grads, ids, lse, along, stat_rows, rows, own, bk=256):
     width = query.shape[1]
-    heads = width // 64
+    heads, bq = width // 64, rows
     return pl.pallas_call(
-        functools.partial(bwd_kernel, bq, bk, own),
+        functools.partial(bwd_kernel, bk, own),
         out_shape=jax.ShapeDtypeStruct((rows, 3 * width), BF16),
-        in_specs=[VMEM] * 8,
+        in_specs=[HBM] * 4 + [VMEM] * 4,
         out_specs=pl.BlockSpec(memory_space=pltpu.VMEM),
-        scratch_shapes=[pltpu.VMEM((heads, bq, 128), F32)] * 3 + [pltpu.VMEM((heads, bq, 128), BF16)] * 4 + [pltpu.VMEM((heads, bq, 128), F32)] * 2 + [pltpu.VMEM((bq, 128), F32)],
-        compiler_params=pltpu.CompilerParams(vmem_limit_bytes=40 << 20),
+        scratch_shapes=[pltpu.VMEM(query.shape, BF16)] * 4 + [pltpu.SemaphoreType.DMA((4, query.shape[0] // bk))] + [pltpu.VMEM((heads, bq, 128), F32)] * 3 + [pltpu.VMEM((heads, bq, 128), BF16)] * 4 + [pltpu.VMEM((heads, bq, 128), F32)] * 2 + [pltpu.VMEM((bq, 128), F32)],
+        compiler_params=pltpu.CompilerParams(vmem_limit_bytes=60 << 20),
         name="attention_backward",
     )(query, key, value, grads, ids, lse, along, stat_rows)
 
@@ -213,9 +240,9 @@
         self.sibling = s + 1 - 2 * self.core
         self.left, self.right = s >= 2, s < count - 2
 
-    def greet(self):
+    def neighbours(self):
         s, count = self.s, self.count
-        greet([(s >= k, {"seq": s - k}) for k in (1, 2)] + [(s < count - k, {"seq": s + k}) for k in (1, 2)])
+        return [(s >= k, {"seq": s - k}) for k in (1, 2)] + [(s < count - k, {"seq": s + k}) for k in (1, 2)]
 
     def own(self, part, kind, slot, target):
         source, window = self.pieces[part]
@@ -280,7 +307,7 @@
 
 
 def project_kernel(count, parts, own_ref, slots_ref, memory_ref, weight_ref, query_bias_ref, value_bias_ref,
-                   q_ref, k_ref, v_ref, source_ref, window_ref, weight, send_sem, recv_sem, local_sem):
+                   q_ref, k_ref, v_ref, source_ref, window_ref, weight, table, send_sem, recv_sem, local_sem):
     block = own_ref.shape[0]
     rows = block // parts
     tile = 256
@@ -290,7 +317,7 @@
         return own_ref.at[pl.ds(part * rows, rows)], lambda slot: window_ref.at[pl.ds(slot * block + part * rows, rows)]
 
     halo = Halo(count, [piece(part) for part in range(parts)], send_sem, recv_sem)
-    halo.greet()
+    greet(halo.neighbours())
     for part in range(parts):
         halo.send(part)
     local = [
@@ -299,12 +326,14 @@
     ]
     for copy in local:
         copy.start()
+    table[...] = jnp.zeros_like(table)
+    table[0:memory_ref.shape[0], :] = memory_ref[...]
     query_bias, value_bias = query_bias_ref[...].reshape(1, -1), value_bias_ref[...].reshape(1, -1)
 
     def project(load, start, keep):
         hot = (lax.broadcasted_iota(jnp.int32, (32, tile), 0) == slots_ref[0:1, pl.ds(start, tile)]).astype(F32).astype(BF16)
         tn = (((0,), (0,)), ((), ()))
-        chosen = dot(hot, memory_ref[...], tn)
+        chosen = dot(hot, table[...], tn)
         inside = wide(dot(hot, jnp.ones((32, 128), BF16), tn), chosen.shape[1])
         source = jnp.where(inside > 0.5, chosen, load().astype(F32)).astype(BF16)
         keep(source)
@@ -363,6 +392,7 @@
         scratch_shapes=[
             pltpu.VMEM((total, dim), BF16),
             pltpu.VMEM(weight.shape, BF16),
+            pltpu.VMEM((32, dim), BF16),
             pltpu.SemaphoreType.DMA((7, parts)),
             pltpu.SemaphoreType.DMA((7, parts)),
             pltpu.SemaphoreType.DMA((2,)),
@@ -370,63 +400,6 @@
         compiler_params=pltpu.CompilerParams(collective_id=collective_id, has_side_effects=True, vmem_limit_bytes=40 << 20),
         name="project_window",
     )(own, slots, memory, weight, query_bias, value_bias)
-
-
-def grads_kernel(count, parts, grad_ref, mixed_ref, lse_ref, low_ref, window_ref, stats_ref, along_ref, out_grad_ref, own_stats, send_sem, recv_sem):
-    block, width = grad_ref.shape
-    rows = block // parts
-
-    def piece(part):
-        return grad_ref.at[pl.ds(part * rows, rows)], lambda slot: window_ref.at[pl.ds(slot * block + part * rows, rows)]
-
-    stats_piece = own_stats, lambda slot: stats_ref.at[:, pl.ds(slot * block, block)]
-    halo = Halo(count, [piece(part) for part in range(parts)] + [stats_piece], send_sem, recv_sem)
-    halo.greet()
-    for part in range(parts):
-        halo.send(part)
-    window_ref[REACH * block:(REACH + 1) * block, :] = grad_ref[...]
-    lane = lax.broadcasted_iota(jnp.int32, (block, 128), 1)
-    along = jnp.zeros((block, 128), F32)
-    for pair in range(width // 128):
-        lanes = slice(pair * 128, pair * 128 + 128)
-        product = grad_ref[:, lanes].astype(F32) * mixed_ref[:, lanes].astype(F32)
-        even = jnp.sum(jnp.where(lane < 64, product, 0.0), axis=1, keepdims=True)
-        odd = jnp.sum(jnp.where(lane < 64, 0.0, product), axis=1, keepdims=True)
-        along = jnp.where(lane == 2 * pair, even, jnp.where(lane == 2 * pair + 1, odd, along))
-    along_ref[...] = along
-    own_stats[0:8, :] = jnp.transpose(lse_ref[...])[0:8, :]
-    own_stats[8:16, :] = jnp.transpose(along)[0:8, :]
-    stats_ref[:, REACH * block:(REACH + 1) * block] = own_stats[...]
-    halo.send(parts)
-    out_grad_ref[...] = dot(low_ref[...], mixed_ref[...], (((0,), (0,)), ((), ()))).astype(BF16)
-    for part in range(parts + 1):
-        halo.relay(part)
-    for slot in (0, 2, 4, 6):
-        halo.receive(slot)
-    halo.finish()
-
-
-def gather_grads(grad, mixed, lse, low, count, collective_id, parts=2):
-    rows, width = grad.shape
-    total = (2 * REACH + 1) * rows
-    return pl.pallas_call(
-        functools.partial(grads_kernel, count, parts),
-        out_shape=(
-            jax.ShapeDtypeStruct((total, width), BF16),
-            jax.ShapeDtypeStruct((16, total), F32),
-            jax.ShapeDtypeStruct((rows, 128), F32),
-            jax.ShapeDtypeStruct((low.shape[1], width), BF16),
-        ),
-        in_specs=[VMEM] * 4,
-        out_specs=(VMEM,) * 4,
-        scratch_shapes=[
-            pltpu.VMEM((16, rows), F32),
-            pltpu.SemaphoreType.DMA((7, parts + 1)),
-            pltpu.SemaphoreType.DMA((7, parts + 1)),
-        ],
-        compiler_params=pltpu.CompilerParams(collective_id=collective_id, has_side_effects=True, vmem_limit_bytes=24 << 20),
-        name="gather_grads",
-    )(grad, mixed, lse, low)
 
 
 def split_dot(left, right, dims):
@@ -755,13 +728,12 @@
 
 
 def feed_kernel(dps, seqs, span, *refs):
-    (mixed_ref, out_ref, other_ref, source_ref, up_hbm, down_hbm, grad_ref), vectors = refs[:7], refs[7:14]
-    share_refs = refs[14:14 + dps]
-    feed_body(dps, seqs, span, mixed_ref, out_ref, other_ref, source_ref, up_hbm, down_hbm, grad_ref, vectors, share_refs, *refs[14 + dps:])
-
-
-def feed_body(dps, seqs, span, mixed_ref, out_ref, other_ref, source_ref, up_hbm, down_hbm, grad_ref, vectors, share_refs,
-                y_ref, input1_ref, low_ref, mixed_grad_ref, small_ref,
+    feed_body(dps, seqs, span, *refs[:8], refs[8:15], refs[15:15 + dps], *refs[15 + dps:])
+
+
+def feed_body(dps, seqs, span, mixed_ref, out_ref, other_ref, source_ref, up_hbm, down_hbm, grad_ref, lse_ref, vectors, share_refs,
+                y_ref, input1_ref, window_ref, stats_ref, along_ref, out_grad_ref, small_ref,
+                low_ref, own_stats, h_send, h_recv,
                 up_ref, down_ref, w_sems, out_all, mixed_all, first_ref, hat_ref, scale_ref, first_low, act_ref, slope_ref, second_ref, down_grad, up_grad,
                 y_send, y_recv, z_send, z_recv, grads, a_recv, m_sems, y_sems, z_sems, a_sems):
     rows, dim = source_ref.shape
@@ -772,7 +744,13 @@
     sibling = s + 1 - 2 * core
     spans = rows // span
     true = s >= 0
-    greet([(true, {"tensor": 1 - t}), (true, {"seq": sibling})])
+
+    def piece(part):
+        return window_ref.at[pl.ds(REACH * rows + part * span, span)], lambda slot: window_ref.at[pl.ds(slot * rows + part * span, span)]
+
+    stats_piece = own_stats, lambda slot: stats_ref.at[:, pl.ds(slot * rows, rows)]
+    halo = Halo(seqs, [piece(part) for part in range(spans)] + [stats_piece], h_send, h_recv)
+    greet([(true, {"tensor": 1 - t})] + halo.neighbours())
     tn = (((0,), (0,)), ((), ()))
 
     def at(i):
@@ -885,7 +863,7 @@
         for j in range(zs):
             a_copy(which, j).start()
 
-    def back(i, carry):
+    def back(i):
         z_copy(i).wait()
         grad = second_ref[at(i), :] + (z_send[at(i), :].astype(F32) + z_recv[at(i), :].astype(F32))
         hat = hat_ref[at(i), :]
@@ -896,10 +874,24 @@
         input1_ref[at(i), :] = total
         low_ref[at(i), :] = low
         add_rows(4, low.astype(F32))
-        mixed_grad_ref[at(i), :] = dot(low, out_ref[...]).astype(BF16)
-        return carry
-
-    lax.fori_loop(0, spans, back, 0)
+        window_ref[REACH * rows + i * span:REACH * rows + (i + 1) * span, :] = dot(low, out_ref[...]).astype(BF16)
+        halo.send(i)
+
+    for i in range(spans):
+        back(i)
+    lane = lax.broadcasted_iota(jnp.int32, (rows, 128), 1)
+    along = jnp.zeros((rows, 128), F32)
+    for pair in range(width // 128):
+        lanes = slice(pair * 128, pair * 128 + 128)
+        product = window_ref[REACH * rows:(REACH + 1) * rows, lanes].astype(F32) * mixed_ref[:, lanes].astype(F32)
+        even = jnp.sum(jnp.where(lane < 64, product, 0.0), axis=1, keepdims=True)
+        odd = jnp.sum(jnp.where(lane < 64, 0.0, product), axis=1, keepdims=True)
+        along = jnp.where(lane == 2 * pair, even, jnp.where(lane == 2 * pair + 1, odd, along))
+    along_ref[...] = along
+    own_stats[0:8, :] = jnp.transpose(lse_ref[...])[0:8, :]
+    own_stats[8:16, :] = jnp.transpose(along)[0:8, :]
+    stats_ref[:, REACH * rows:(REACH + 1) * rows] = own_stats[...]
+    halo.send(spans)
     share = 2 * hidden // dps
     for which in range(2):
         for j in range(zs):
@@ -916,25 +908,39 @@
                         def _():
                             share_refs[k][j, :, first - p * share:last - p * share] = total.astype(BF16)
 
-
-def feed_forward(mixed, out_weight, out_other, source, up, down, vectors, grad, dps, seqs, span=256):
+    out_grad_ref[...] = dot(low_ref[...], mixed_ref[...], tn).astype(BF16)
+    for part in range(spans + 1):
+        halo.relay(part)
+    for slot in (0, 2, 4, 6):
+        halo.receive(slot)
+    halo.finish()
+
+
+def feed_forward(mixed, out_weight, out_other, source, up, down, grad, lse, vectors, dps, seqs, span=256):
     rows, dim = source.shape
     width, hidden = mixed.shape[1], up.shape[1]
     zs, block = seqs // 2, dim // seqs
     spans = rows // span
+    total = (2 * REACH + 1) * rows
     dma = pltpu.SemaphoreType.DMA
     return pl.pallas_call(
         functools.partial(feed_kernel, dps, seqs, span),
         out_shape=(jax.ShapeDtypeStruct((zs, block, 2 * hidden // dps), BF16),) * dps + (
             jax.ShapeDtypeStruct((rows, dim), BF16),
             jax.ShapeDtypeStruct((rows, dim), F32),
-            jax.ShapeDtypeStruct((rows, dim), BF16),
-            jax.ShapeDtypeStruct((rows, width), BF16),
+            jax.ShapeDtypeStruct((total, width), BF16),
+            jax.ShapeDtypeStruct((16, total), F32),
+            jax.ShapeDtypeStruct((rows, 128), F32),
+            jax.ShapeDtypeStruct((dim, width), BF16),
             jax.ShapeDtypeStruct((8, dim), F32),
         ),
-        in_specs=[VMEM] * 4 + [HBM] * 2 + [VMEM] * 8,
-        out_specs=(VMEM,) * (dps + 5),
+        in_specs=[VMEM] * 4 + [HBM] * 2 + [VMEM] * 9,
+        out_specs=(VMEM,) * (dps + 7),
         scratch_shapes=[
+            pltpu.VMEM((rows, dim), BF16),
+            pltpu.VMEM((16, rows), F32),
+            dma((7, spans + 1)),
+            dma((7, spans + 1)),
             pltpu.VMEM((dim, hidden), BF16),
             pltpu.VMEM((dim, hidden), BF16),
             dma((2,)),
@@ -962,7 +968,7 @@
         ],
         compiler_params=pltpu.CompilerParams(collective_id=3, has_side_effects=True, vmem_limit_bytes=56 << 20),
         name="feed_forward",
-    )(mixed, out_weight, out_other, source, up, down, grad, *vectors)
+    )(mixed, out_weight, out_other, source, up, down, grad, lse, *vectors)
 
 
 def memory_slots(id_row):
@@ -992,20 +998,18 @@
     out_other = lax.ppermute(out_weight, "tensor", [(0, 1), (1, 0)])
     weight = qkv_weight.transpose(1, 0, 2)
     slots_row = jnp.broadcast_to(window_slots[None], (8, pieces * rows))
-    memory_pad = jnp.pad(memory, ((0, 32 - memory.shape[0]), (0, 0)))
     query, key, value, source = project_window(
-        tokens[0], slots_row, memory_pad, weight, query_bias, value_bias, seqs, 1)
+        tokens[0], slots_row, memory, weight, query_bias, value_bias, seqs, 1)
     own_slots = window_slots[own:own + rows]
 
     mixed_low, logsums = attention_forward(query, key, value, ids, rows, own, bq, bk)
 
     vectors = (out_bias, norm1_gain, norm1_bias, down_bias, norm2_gain, norm2_bias, up_bias)
-    *shares, output, grad_input1, branch_grad, mixed_grad, small = feed_forward(
-        mixed_low, out_weight, out_other, source, up_weight, down_weight, vectors, out_grad[0], dps, seqs)
+    *shares, output, grad_input1, grads_window, stats_window, along_cols, grad_out_weight, small = feed_forward(
+        mixed_low, out_weight, out_other, source, up_weight, down_weight, out_grad[0], logsums, vectors, dps, seqs)
     early = shares[:1] + [
         lax.ppermute(shares[k], "dp", [(i, (i + k) % dps) for i in range(dps)]) for k in range(1, dps)]
-    grads_window, stats_window, along_cols, grad_out_weight = gather_grads(mixed_grad, mixed_low, logsums, branch_grad, seqs, 2)
-    proj_grad = attention_backward(query, key, value, grads_window, ids, logsums, along_cols, stats_window, rows, own, bq, bk)
+    proj_grad = attention_backward(query, key, value, grads_window, ids, logsums, along_cols, stats_window, rows, own, bk)
 
     select = (own_slots[:, None] == jnp.arange(32, dtype=jnp.int32)[None, :]).astype(BF16)
     up_sum, down_sum, out_sum, qkv_sum, input_grad, small = tail(

time: 221 us -> 217 us (0.982)
  Pallas kernels: 193 us -> 182 us
  waiting for transfers between devices: 0.01 us -> 10.4 us
    pallas_call x2 -> x1, Pallas kernels: 33.7 us -> 15.9 us  [attention_backward(): pl.pallas_call(functools.partial(bwd_kernel, bk, own), out_shape=jax.Shap...]
    pallas_call x1, Pallas kernels: 56 us -> 72.9 us  [feed_forward(): pl.pallas_call(functools.partial(feed_kernel, dps, seqs, span), out_shape...]
    ppermute x1, waiting for transfers between devices: 0.01 us -> 10.4 us  [on_device(): lax.ppermute(shares[k], 'dp', [(i, (i + k) % dps) for i in range(dps)])]
    pallas_call x1, Pallas kernels: 69.8 us -> 59.7 us  [tail(): pl.pallas_call(functools.partial(tail_kernel, dps, seqs, width), out_shap...]
    unnamed x42 -> x52, local copies, waits for them, and re-layouts: 16.2 us -> 16.1 us
  transfers between devices with their start and end apart: 2 -> 2, of which waited for: 0 -> 1; matrix products, arithmetic and copies ran while one was open for 2% -> 1% of each run, Pallas kernels for 30% -> 23%
where the time goes in v2:
time: 217 us; the launch traced here: 218 us
  Pallas kernels  182 us (84%)
  local copies, waits for them, and re-layouts  18.6 us (9%)
  waiting for transfers between devices  10.4 us (5%)
  starting transfers between devices  3.13 us (1%)
  other arithmetic  2.59 us (1%)
    pallas_call x1, Pallas kernels, feed_forward(): pl.pallas_call(functools.partial(feed_kernel, dps, seqs, span), out_shape...  72.9 us
    pallas_call x1, Pallas kernels, tail(): pl.pallas_call(functools.partial(tail_kernel, dps, seqs, width), out_shap...  59.7 us
    pallas_call x1, Pallas kernels, project_window(): pl.pallas_call(functools.partial(project_kernel, count, parts), out_shape...  27.8 us
    unnamed x52, local copies, waits for them, and re-layouts  16.1 us
    pallas_call x1, Pallas kernels, attention_backward(): pl.pallas_call(functools.partial(bwd_kernel, bk, own), out_shape=jax.Shap...  15.9 us
    ppermute x1, waiting for transfers between devices, on_device(): lax.ppermute(shares[k], 'dp', [(i, (i + k) % dps) for i in range(dps)])  10.4 us
    pallas_call x1, Pallas kernels, attention_forward(): pl.pallas_call(functools.partial(fwd_kernel, bq, bk, own), out_shape=(jax...  5.5 us
  transfers between devices with their start and end apart: 2, of which 1 were waited for; matrix products, arithmetic and copies ran while one was open for 1% of the time, Pallas kernels for 23%

profile of v2, /device:TPU:0, one launch (start us, length us, event | category | flops | bytes accessed | tf_op | source)
XLA Modules:
  0.0 217.5 jit_solution(11760623787822920339)
XLA Ops:
  0.6 3.1 %collective-permute-start = (bf16[768,384]{1,0:T(8,128)(2,1)}, bf16[768,384]{1,0:T(8,128)(2,1)S(1)}, u32[]{:S(2)}, u32[]{:S(2)}) collective-permute-start(bf16[768,384]{1,0:T(8,128)(2,1)} %refs_1_.1), channel_id=1, source_target_pairs={{0,1},{1,0},{2,3},{3,2},{4,5},{5,4},{6,7},{7,6},{8,9},{9,8},{10,11... | collective-permute-start | bytes 1769480 | tf_op jit(solution)/shard_map/ppermute | solution.py:998
  3.7 1.6 compare_select_fusion
  5.4 0.8 fusion.5
  6.2 0.0 copy-start.3
  6.2 1.5 copy-done.3
  7.7 0.0 copy-start.9
  7.7 1.1 copy-done.9
  8.8 0.8 copy-done.18
  9.6 0.0 copy-start.20
  9.6 0.7 copy-done.20
  10.3 0.0 copy-start.21
  10.3 0.7 copy-done.21
  11.0 27.8 %project_window.1 = (bf16[3584,384]{1,0:T(8,128)(2,1)S(1)}, bf16[3584,384]{1,0:T(8,128)(2,1)S(1)}, bf16[3584,384]{1,0:T(8,128)(2,1)S(1)}, bf16[512,768]{1,0:T(8,128)(2,1)S(1)}) custom-call(bf16[512,768]{1,0:T(8,128)(2,1)S(1)} %bitcast.23, s32[8,3584]{1,0:T(8,128)S(1)} %broadcast_in_dim.32.slots_ref, bf16[20,768]{1,0:T(8,128)(2,1)S(1)} %copy-done.18, ...), custom_call_target="tpu_custom_call" | custom-call | tf_op jit(solution)/shard_map/project_window/pallas_call | solution.py:387
  38.8 0.0 copy-start.4
  38.8 0.9 copy-done.4
  39.7 0.0 copy-start
  39.7 0.0 copy-start.1
  39.7 0.0 copy-start.2
  39.7 0.0 copy-start.8
  39.7 5.5 %attention_forward.1 = (bf16[512,384]{1,0:T(8,128)(2,1)S(1)}, f32[512,128]{1,0:T(8,128)S(1)}) custom-call(bf16[3584,384]{1,0:T(8,128)(2,1)S(1)} %get-tuple-element.37.q_ref.q_hbm, bf16[3584,384]{1,0:T(8,128)(2,1)S(1)} %get-tuple-element.38.k_ref.k_hbm, bf16[3584,384]{1,0:T(8,128)(2,1)S(1)} %get-tuple-element.39.v_ref.v_hbm, ...), custom_call_target="tpu_custom_call" | custom-call | tf_op jit(solution)/shard_map/attention_forward/pallas_call | solution.py:136
  45.2 0.0 copy-done
  45.2 0.0 copy-done.1
  45.2 0.0 copy-done.2
  45.2 0.0 copy-done.8
  45.2 0.0 copy-start.7
  45.3 0.7 copy-done.7
  45.9 0.0 copy-start.15
  45.9 0.7 copy-done.15
  46.7 0.0 collective-permute-done.refs_2_
  46.7 0.0 copy-start.22
  46.7 0.8 copy-done.22
  47.5 72.9 %feed_forward.1 = (bf16[4,96,1536]{2,1,0:T(8,128)(2,1)}, bf16[4,96,1536]{2,1,0:T(8,128)(2,1)}, bf16[512,768]{1,0:T(8,128)(2,1)}, f32[512,768]{1,0:T(8,128)}, bf1...) custom-call(bf16[512,384]{1,0:T(8,128)(2,1)} %copy-done.15, ...), custom_call_target="tpu_custom_call" | custom-call | tf_op jit(solution)/shard_map/feed_forward/pallas_call | solution.py:926
  120.4 0.1 collective-permute-start.1
  120.5 0.1 fusion.refs_7_
  120.6 0.0 copy-start.5
  120.7 0.0 copy-start.6
  120.7 0.0 copy-start.10
  120.7 0.0 copy-start.19
  120.7 15.9 %attention_backward.1.refs_3_ = bf16[512,1152]{1,0:T(8,128)(2,1)} custom-call(bf16[3584,384]{1,0:T(8,128)(2,1)} %copy-done, bf16[3584,384]{1,0:T(8,128)(2,1)} %copy-done.1, bf16[3584,384]{1,0:T(8,128)(2,1)} %copy-done.2, bf16[3584,384]{1,0:T(8,128)(2,1)} %get-tuple-element.47.g_hbm, f32[8,3584]{1,0:T(8,128)} %copy-done.8, f32[512,128]{1,0:T(8,128)} %copy-done.7, ...), custom_call_target="tpu_custom_call" | custom-call | tf_op jit(solution)/shard_map/attention_backward/pallas_call | solution.py:225
  136.6 10.4 %collective-permute-done.1.refs_1_ = bf16[4,96,1536]{2,1,0:T(8,128)(2,1)} collective-permute-done((bf16[4,96,1536]{2,1,0:T(8,128)(2,1)}, bf16[4,96,1536]{2,1,0:T(8,128)(2,1)}, u32[]{:S(2)}, u32[]{:S(2)}) %collective-permute-start.1) | collective-permute-done | bytes 1179680 | tf_op jit(solution)/shard_map/ppermute | solution.py:1011
  147.1 0.0 copy-done.5
  147.1 0.0 copy-done.6
  147.1 0.0 copy-done.10
  147.1 0.0 copy-done.19
  147.1 59.7 %tail.1 = (f32[96,1536]{1,0:T(8,128)S(1)}, f32[96,1536]{1,0:T(8,128)S(1)}, f32[96,384]{1,0:T(8,128)S(1)}, f32[3,96,384]{2,1,0:T(8,128)S(1)}, bf16[512,768]{1,0:T(8,128)(2,1)S(1)}, /*index=5*/f32[4,8,768]{2,1,0:T(8,128)S(1)}) custom-call(bf16[4,96,1536]{2,1,0:T(8,128)(2,1)S(1)} %copy-done.6, bf16[4,96,1536]{2,1,0:T(8,128)(2,1)} %collective-permute-done.1.refs_1_, ...), custom_call_target="tpu_custom_call" | custom-call | tf_op jit(solution)/shard_map/tail/pallas_call | solution.py:691
  206.8 0.0 copy-start.11
  206.8 0.8 copy-done.11
  207.6 0.0 copy-start.13
  207.6 0.8 copy-done.13
  208.4 0.7 copy-done.16
  209.0 0.6 slice.149
  209.7 0.6 slice_reduce_fusion
  210.3 0.1 constant_dynamic-slice_fusion
  210.4 0.5 slice_bitcast_fusion
  210.9 0.6 reshape.42
  211.5 2.1 copy.39
  213.6 0.9 copy.40
  214.5 0.0 copy-done.14
  214.5 0.8 copy.41
  215.2 0.0 copy-done.17
  215.2 0.7 copy.42
  215.9 0.0 copy-done.12
  215.9 0.8 copy.43
  216.7 0.8 copy.44
  (12 shorter events, 0.0 us)
Async XLA Ops:
  0.6 46.0 %collective-permute-start = (bf16[768,384]{1,0:T(8,128)(2,1)}, bf16[768,384]{1,0:T(8,128)(2,1)S(1)}, u32[]{:S(2)}, u32[]{:S(2)}) collective-permute-start(bf16[768,384]{1,0:T(8,128)(2,1)} %refs_1_.1), channel_id=1, source_target_pairs={{0,1},{1,0},{2,3},{3,2},{4,5},{5,4},{6,7},{7,6},{8,9},{9,8},{10,11... | collective-permute-start | bytes 1769480 | tf_op jit(solution)/shard_map/ppermute | solution.py:998
  6.2 1.5 copy-start.3
  7.7 1.1 copy-start.9
  8.8 0.8 copy-start.18
  9.6 0.7 copy-start.20
  10.3 0.7 copy-start.21
  38.8 0.9 copy-start.4
  39.7 5.5 %copy-start = (bf16[3584,384]{1,0:T(8,128)(2,1)}, bf16[3584,384]{1,0:T(8,128)(2,1)S(1)}, u32[]{:S(2)}) copy-start(bf16[3584,384]{1,0:T(8,128)(2,1)S(1)} %get-tuple-element.37.q_ref.q_hbm) | copy-start | bytes 8257540
  39.7 5.5 %copy-start.1 = (bf16[3584,384]{1,0:T(8,128)(2,1)}, bf16[3584,384]{1,0:T(8,128)(2,1)S(1)}, u32[]{:S(2)}) copy-start(bf16[3584,384]{1,0:T(8,128)(2,1)S(1)} %get-tuple-element.38.k_ref.k_hbm) | copy-start | bytes 8257540
  39.7 5.6 %copy-start.2 = (bf16[3584,384]{1,0:T(8,128)(2,1)}, bf16[3584,384]{1,0:T(8,128)(2,1)S(1)}, u32[]{:S(2)}) copy-start(bf16[3584,384]{1,0:T(8,128)(2,1)S(1)} %get-tuple-element.39.v_ref.v_hbm) | copy-start | bytes 8257540
  39.7 5.5 %copy-start.8 = (f32[8,3584]{1,0:T(8,128)}, f32[8,3584]{1,0:T(8,128)S(1)}, u32[]{:S(2)}) copy-start(f32[8,3584]{1,0:T(8,128)S(1)} %broadcast_in_dim.34.ids_ref) | copy-start | bytes 344068
  45.2 0.7 copy-start.7
  45.9 0.7 copy-start.15
  46.7 0.8 copy-start.22
  120.4 26.7 %collective-permute-start.1 = (bf16[4,96,1536]{2,1,0:T(8,128)(2,1)}, bf16[4,96,1536]{2,1,0:T(8,128)(2,1)}, u32[]{:S(2)}, u32[]{:S(2)}) collective-permute-start(bf16[4,96,1536]{2,1,0:T(8,128)(2,1)} %get-tuple-element.45), channel_id=1, source_target_pairs={{0,16},{16,0},{1,17},{17,1},{2,18},{18,2},{3,19},{19,3},{4,20},{20... | collective-permute-start | bytes 3538952 | tf_op jit(solution)/shard_map/ppermute | solution.py:1011
  120.6 26.4 %copy-start.5 = (bf16[512,768]{1,0:T(8,128)(2,1)S(1)}, bf16[512,768]{1,0:T(8,128)(2,1)}, u32[]{:S(2)}) copy-start(bf16[512,768]{1,0:T(8,128)(2,1)} %copy-done.4) | copy-start | bytes 2359300
  120.7 26.4 %copy-start.6 = (bf16[4,96,1536]{2,1,0:T(8,128)(2,1)S(1)}, bf16[4,96,1536]{2,1,0:T(8,128)(2,1)}, u32[]{:S(2)}) copy-start(bf16[4,96,1536]{2,1,0:T(8,128)(2,1)} %get-tuple-element.44.refs_0_) | copy-start | bytes 3538948
  120.7 26.4 %copy-start.10 = (bf16[768,384]{1,0:T(8,128)(2,1)S(1)}, bf16[768,384]{1,0:T(8,128)(2,1)}, u32[]{:S(2)}) copy-start(bf16[768,384]{1,0:T(8,128)(2,1)} %get-tuple-element.46.refs_2_) | copy-start | bytes 1769476
  120.7 26.4 %copy-start.19 = (f32[8,768]{1,0:T(8,128)S(1)}, f32[8,768]{1,0:T(8,128)}, u32[]{:S(2)}) copy-start(f32[8,768]{1,0:T(8,128)} %get-tuple-element.51.refs_8_) | copy-start | bytes 73732
  206.8 0.8 copy-start.11
  207.6 0.8 copy-start.13
  208.4 0.7 copy-start.16
  209.0 5.4 %copy-start.14 = (f32[3,96,384]{2,1,0:T(8,128)S(1)}, f32[3,96,384]{2,1,0:T(8,128)}, u32[]{:S(2)}) copy-start(f32[3,96,384]{2,1,0:T(8,128)} %copy-done.13) | copy-start | bytes 1327108
  209.0 6.2 %copy-start.17 = (f32[96,384]{1,0:T(8,128)S(1)}, f32[96,384]{1,0:T(8,128)}, u32[]{:S(2)}) copy-start(f32[96,384]{1,0:T(8,128)} %copy-done.16) | copy-start | bytes 442372
  209.0 6.8 %copy-start.12 = (f32[96,1536]{1,0:T(8,128)S(1)}, f32[96,1536]{1,0:T(8,128)}, u32[]{:S(2)}) copy-start(f32[96,1536]{1,0:T(8,128)} %copy-done.11) | copy-start | bytes 1769476

commit v3 on v2

--- a/solution.py
+++ b/solution.py
@@ -971,10 +971,8 @@
     )(mixed, out_weight, out_other, source, up, down, grad, lse, *vectors)
 
 
-def memory_slots(id_row):
-    count = id_row.shape[0]
-    edge = jnp.full((READ_ROWS,), -1, jnp.int32)
-    padded = jnp.concatenate([edge, id_row, edge])
+def memory_slots(padded, count):
+    id_row = padded[READ_ROWS:READ_ROWS + count]
     before = sum((padded[READ_ROWS - k:READ_ROWS - k + count] == id_row).astype(jnp.int32) for k in range(1, READ_ROWS + 1))
     behind = sum((padded[READ_ROWS + k:READ_ROWS + k + count] == id_row).astype(jnp.int32) for k in range(1, READ_ROWS + 1))
     return jnp.where(before < READ_ROWS, before, jnp.where(behind < READ_ROWS, 2 * READ_ROWS - 1 - behind, -1))
@@ -989,10 +987,11 @@
     pieces = 2 * REACH + 1
     s = lax.axis_index("seq")
     id_row = doc_ids[0]
-    edge = jnp.full((own,), -1, jnp.int32)
-    slots = memory_slots(id_row)
-    window_slots = lax.dynamic_slice_in_dim(jnp.concatenate([edge, slots, edge]), s * rows, pieces * rows, 0)
-    window_ids = lax.dynamic_slice_in_dim(jnp.concatenate([edge, id_row, jnp.full((own,), 1 << 20, jnp.int32)]), s * rows, pieces * rows, 0)
+    edge = (own + READ_ROWS,)
+    padded = lax.dynamic_slice_in_dim(
+        jnp.concatenate([jnp.full(edge, -1, jnp.int32), id_row, jnp.full(edge, 1 << 20, jnp.int32)]), s * rows, pieces * rows + 2 * READ_ROWS, 0)
+    window_slots = memory_slots(padded, pieces * rows)
+    window_ids = padded[READ_ROWS:READ_ROWS + pieces * rows]
     ids = jnp.broadcast_to(window_ids.astype(F32)[None], (8, pieces * rows))
 
     out_other = lax.ppermute(out_weight, "tensor", [(0, 1), (1, 0)])

time: 217 us -> 215 us (level); the launches traced: 218 us -> 211 us
  Pallas kernels: 182 us -> 177 us
    pallas_call x1, Pallas kernels: 72.9 us -> 69.6 us  [feed_forward(): pl.pallas_call(functools.partial(feed_kernel, dps, seqs, span), out_shape...]
where the time goes in v3:
time: 215 us; the launch traced here: 211 us
  Pallas kernels  177 us (82%)
  local copies, waits for them, and re-layouts  19.4 us (9%)
  waiting for transfers between devices  9.94 us (5%)
  starting transfers between devices  3.13 us (1%)
    pallas_call x1, Pallas kernels, feed_forward(): pl.pallas_call(functools.partial(feed_kernel, dps, seqs, span), out_shape...  69.6 us
    pallas_call x1, Pallas kernels, tail(): pl.pallas_call(functools.partial(tail_kernel, dps, seqs, width), out_shap...  58.1 us
    pallas_call x1, Pallas kernels, project_window(): pl.pallas_call(functools.partial(project_kernel, count, parts), out_shape...  27.8 us
    unnamed x52, local copies, waits for them, and re-layouts  16.1 us
    pallas_call x1, Pallas kernels, attention_backward(): pl.pallas_call(functools.partial(bwd_kernel, bk, own), out_shape=jax.Shap...  15.9 us
    ppermute x1, waiting for transfers between devices, on_device(): lax.ppermute(shares[k], 'dp', [(i, (i + k) % dps) for i in range(dps)])  9.94 us
    pallas_call x1, Pallas kernels, attention_forward(): pl.pallas_call(functools.partial(fwd_kernel, bq, bk, own), out_shape=(jax...  5.58 us
  transfers between devices with their start and end apart: 2, of which 1 were waited for; matrix products, arithmetic and copies ran while one was open for 1% of the time, Pallas kernels for 23%

profile of v3, /device:TPU:0, one launch (start us, length us, event | category | flops | bytes accessed | tf_op | source)
XLA Modules:
  0.0 210.8 jit_solution(10295159941948104729)
XLA Ops:
  0.6 3.1 %collective-permute-start = (bf16[768,384]{1,0:T(8,128)(2,1)}, bf16[768,384]{1,0:T(8,128)(2,1)S(1)}, u32[]{:S(2)}, u32[]{:S(2)}) collective-permute-start(bf16[768,384]{1,0:T(8,128)(2,1)} %refs_1_.1), channel_id=1, source_target_pairs={{0,1},{1,0},{2,3},{3,2},{4,5},{5,4},{6,7},{7,6},{8,9},{9,8},{10,11... | collective-permute-start | bytes 1769480 | tf_op jit(solution)/shard_map/ppermute | solution.py:997
  3.7 0.8 concatenate.3
  4.5 0.3 compare_select_fusion
  4.8 0.0 copy-start.3
  4.8 1.5 copy-done.3
  6.3 0.0 copy-start.9
  6.3 1.1 copy-done.9
  7.4 0.0 copy-start.18
  7.4 0.8 copy-done.18
  8.2 0.0 copy-start.20
  8.2 0.7 copy-done.20
  8.9 0.0 copy-start.21
  8.9 0.7 copy-done.21
  9.5 27.8 %project_window.1 = (bf16[3584,384]{1,0:T(8,128)(2,1)S(1)}, bf16[3584,384]{1,0:T(8,128)(2,1)S(1)}, bf16[3584,384]{1,0:T(8,128)(2,1)S(1)}, bf16[512,768]{1,0:T(8,128)(2,1)S(1)}) custom-call(bf16[512,768]{1,0:T(8,128)(2,1)S(1)} %bitcast.23, s32[8,3584]{1,0:T(8,128)S(1)} %broadcast_in_dim.33.slots_ref, bf16[20,768]{1,0:T(8,128)(2,1)S(1)} %copy-done.18, ...), custom_call_target="tpu_custom_call" | custom-call | tf_op jit(solution)/shard_map/project_window/pallas_call | solution.py:387
  37.4 0.0 copy-start.4
  37.4 0.9 copy-done.4
  38.2 0.0 copy-start
  38.3 0.0 copy-start.1
  38.3 0.0 copy-start.2
  38.3 0.1 dynamic-slice_convert_fusion
  38.3 0.0 copy-start.8
  38.4 5.6 %attention_forward.1 = (bf16[512,384]{1,0:T(8,128)(2,1)S(1)}, f32[512,128]{1,0:T(8,128)S(1)}) custom-call(bf16[3584,384]{1,0:T(8,128)(2,1)S(1)} %get-tuple-element.37.q_ref.q_hbm, bf16[3584,384]{1,0:T(8,128)(2,1)S(1)} %get-tuple-element.38.k_ref.k_hbm, bf16[3584,384]{1,0:T(8,128)(2,1)S(1)} %get-tuple-element.39.v_ref.v_hbm, ...), custom_call_target="tpu_custom_call" | custom-call | tf_op jit(solution)/shard_map/attention_forward/pallas_call | solution.py:136
  43.9 0.0 copy-done
  44.0 0.0 copy-done.1
  44.0 0.0 copy-done.2
  44.0 0.0 copy-done.8
  44.0 0.0 copy-start.7
  44.0 0.7 copy-done.7
  44.7 0.0 copy-start.15
  44.7 0.7 copy-done.15
  45.4 0.0 collective-permute-done.refs_2_
  45.4 0.8 copy-done.22
  46.3 69.6 %feed_forward.1 = (bf16[4,96,1536]{2,1,0:T(8,128)(2,1)}, bf16[4,96,1536]{2,1,0:T(8,128)(2,1)}, bf16[512,768]{1,0:T(8,128)(2,1)}, f32[512,768]{1,0:T(8,128)}, bf1...) custom-call(bf16[512,384]{1,0:T(8,128)(2,1)} %copy-done.15, ...), custom_call_target="tpu_custom_call" | custom-call | tf_op jit(solution)/shard_map/feed_forward/pallas_call | solution.py:926
  115.9 0.1 collective-permute-start.1
  116.0 0.1 fusion.refs_7_
  116.1 0.0 copy-start.5
  116.1 0.0 copy-start.6
  116.1 0.0 copy-start.10
  116.1 0.0 copy-start.19
  116.1 15.9 %attention_backward.1.refs_3_ = bf16[512,1152]{1,0:T(8,128)(2,1)} custom-call(bf16[3584,384]{1,0:T(8,128)(2,1)} %copy-done, bf16[3584,384]{1,0:T(8,128)(2,1)} %copy-done.1, bf16[3584,384]{1,0:T(8,128)(2,1)} %copy-done.2, bf16[3584,384]{1,0:T(8,128)(2,1)} %get-tuple-element.47.g_hbm, f32[8,3584]{1,0:T(8,128)} %copy-done.8, f32[512,128]{1,0:T(8,128)} %copy-done.7, ...), custom_call_target="tpu_custom_call" | custom-call | tf_op jit(solution)/shard_map/attention_backward/pallas_call | solution.py:225
  132.1 9.9 %collective-permute-done.1.refs_1_ = bf16[4,96,1536]{2,1,0:T(8,128)(2,1)} collective-permute-done((bf16[4,96,1536]{2,1,0:T(8,128)(2,1)}, bf16[4,96,1536]{2,1,0:T(8,128)(2,1)}, u32[]{:S(2)}, u32[]{:S(2)}) %collective-permute-start.1) | collective-permute-done | bytes 1179680 | tf_op jit(solution)/shard_map/ppermute | solution.py:1010
  142.0 0.0 copy-done.5
  142.0 0.0 copy-done.6
  142.0 0.0 copy-done.10
  142.0 0.0 copy-done.19
  142.0 58.1 %tail.1 = (f32[96,1536]{1,0:T(8,128)S(1)}, f32[96,1536]{1,0:T(8,128)S(1)}, f32[96,384]{1,0:T(8,128)S(1)}, f32[3,96,384]{2,1,0:T(8,128)S(1)}, bf16[512,768]{1,0:T(8,128)(2,1)S(1)}, /*index=5*/f32[4,8,768]{2,1,0:T(8,128)S(1)}) custom-call(bf16[4,96,1536]{2,1,0:T(8,128)(2,1)S(1)} %copy-done.6, bf16[4,96,1536]{2,1,0:T(8,128)(2,1)} %collective-permute-done.1.refs_1_, ...), custom_call_target="tpu_custom_call" | custom-call | tf_op jit(solution)/shard_map/tail/pallas_call | solution.py:691
  200.1 0.0 copy-start.11
  200.1 0.8 copy-done.11
  200.9 0.8 copy-done.13
  201.7 0.7 copy-done.16
  202.4 0.6 slice.134
  203.0 0.6 slice_reduce_fusion
  203.6 0.1 constant_dynamic-slice_fusion
  203.7 0.5 slice_bitcast_fusion
  204.2 0.6 reshape.42
  204.8 2.1 copy.39
  206.9 0.9 copy.40
  207.8 0.0 copy-done.14
  207.8 0.8 copy.41
  208.5 0.0 copy-done.17
  208.5 0.7 copy.42
  209.2 0.0 copy-done.12
  209.2 0.8 copy.43
  210.0 0.8 copy.44
  (13 shorter events, 0.0 us)
Async XLA Ops:
  0.6 44.8 %collective-permute-start = (bf16[768,384]{1,0:T(8,128)(2,1)}, bf16[768,384]{1,0:T(8,128)(2,1)S(1)}, u32[]{:S(2)}, u32[]{:S(2)}) collective-permute-start(bf16[768,384]{1,0:T(8,128)(2,1)} %refs_1_.1), channel_id=1, source_target_pairs={{0,1},{1,0},{2,3},{3,2},{4,5},{5,4},{6,7},{7,6},{8,9},{9,8},{10,11... | collective-permute-start | bytes 1769480 | tf_op jit(solution)/shard_map/ppermute | solution.py:997
  4.8 1.5 copy-start.3
  6.3 1.1 copy-start.9
  7.4 0.8 copy-start.18
  8.2 0.7 copy-start.20
  8.9 0.7 copy-start.21
  37.4 0.9 copy-start.4
  38.2 5.7 %copy-start = (bf16[3584,384]{1,0:T(8,128)(2,1)}, bf16[3584,384]{1,0:T(8,128)(2,1)S(1)}, u32[]{:S(2)}) copy-start(bf16[3584,384]{1,0:T(8,128)(2,1)S(1)} %get-tuple-element.37.q_ref.q_hbm) | copy-start | bytes 8257540
  38.3 5.7 %copy-start.1 = (bf16[3584,384]{1,0:T(8,128)(2,1)}, bf16[3584,384]{1,0:T(8,128)(2,1)S(1)}, u32[]{:S(2)}) copy-start(bf16[3584,384]{1,0:T(8,128)(2,1)S(1)} %get-tuple-element.38.k_ref.k_hbm) | copy-start | bytes 8257540
  38.3 5.7 %copy-start.2 = (bf16[3584,384]{1,0:T(8,128)(2,1)}, bf16[3584,384]{1,0:T(8,128)(2,1)S(1)}, u32[]{:S(2)}) copy-start(bf16[3584,384]{1,0:T(8,128)(2,1)S(1)} %get-tuple-element.39.v_ref.v_hbm) | copy-start | bytes 8257540
  38.3 5.6 %copy-start.8 = (f32[8,3584]{1,0:T(8,128)}, f32[8,3584]{1,0:T(8,128)S(1)}, u32[]{:S(2)}) copy-start(f32[8,3584]{1,0:T(8,128)S(1)} %broadcast_in_dim.34.ids_ref) | copy-start | bytes 344068
  44.0 0.7 copy-start.7
  44.7 0.7 copy-start.15
  45.4 0.8 copy-start.22
  115.9 26.1 %collective-permute-start.1 = (bf16[4,96,1536]{2,1,0:T(8,128)(2,1)}, bf16[4,96,1536]{2,1,0:T(8,128)(2,1)}, u32[]{:S(2)}, u32[]{:S(2)}) collective-permute-start(bf16[4,96,1536]{2,1,0:T(8,128)(2,1)} %get-tuple-element.45), channel_id=1, source_target_pairs={{0,16},{16,0},{1,17},{17,1},{2,18},{18,2},{3,19},{19,3},{4,20},{20... | collective-permute-start | bytes 3538952 | tf_op jit(solution)/shard_map/ppermute | solution.py:1010
  116.1 25.9 %copy-start.5 = (bf16[512,768]{1,0:T(8,128)(2,1)S(1)}, bf16[512,768]{1,0:T(8,128)(2,1)}, u32[]{:S(2)}) copy-start(bf16[512,768]{1,0:T(8,128)(2,1)} %copy-done.4) | copy-start | bytes 2359300
  116.1 25.9 %copy-start.6 = (bf16[4,96,1536]{2,1,0:T(8,128)(2,1)S(1)}, bf16[4,96,1536]{2,1,0:T(8,128)(2,1)}, u32[]{:S(2)}) copy-start(bf16[4,96,1536]{2,1,0:T(8,128)(2,1)} %get-tuple-element.44.refs_0_) | copy-start | bytes 3538948
  116.1 25.9 %copy-start.10 = (bf16[768,384]{1,0:T(8,128)(2,1)S(1)}, bf16[768,384]{1,0:T(8,128)(2,1)}, u32[]{:S(2)}) copy-start(bf16[768,384]{1,0:T(8,128)(2,1)} %get-tuple-element.46.refs_2_) | copy-start | bytes 1769476
  116.1 25.9 %copy-start.19 = (f32[8,768]{1,0:T(8,128)S(1)}, f32[8,768]{1,0:T(8,128)}, u32[]{:S(2)}) copy-start(f32[8,768]{1,0:T(8,128)} %get-tuple-element.51.refs_8_) | copy-start | bytes 73732
  200.1 0.8 copy-start.11
  200.9 0.8 copy-start.13
  201.7 0.7 copy-start.16
  202.4 5.4 %copy-start.14 = (f32[3,96,384]{2,1,0:T(8,128)S(1)}, f32[3,96,384]{2,1,0:T(8,128)}, u32[]{:S(2)}) copy-start(f32[3,96,384]{2,1,0:T(8,128)} %copy-done.13) | copy-start | bytes 1327108
  202.4 6.2 %copy-start.17 = (f32[96,384]{1,0:T(8,128)S(1)}, f32[96,384]{1,0:T(8,128)}, u32[]{:S(2)}) copy-start(f32[96,384]{1,0:T(8,128)} %copy-done.16) | copy-start | bytes 442372
  202.4 6.8 %copy-start.12 = (f32[96,1536]{1,0:T(8,128)S(1)}, f32[96,1536]{1,0:T(8,128)}, u32[]{:S(2)}) copy-start(f32[96,1536]{1,0:T(8,128)} %copy-done.11) | copy-start | bytes 1769476
